TPU v7x, 128 devices: a whole 4x4x4 slice. The times are simulated.
128 devices in a mesh: row: 32 (over z, x, core), blk: 4 (over y).
Axes of the slice: x: 4, y: 4, z: 4, core: 2. Of those that a mesh axis runs over, the one named last changes fastest.
Arguments:
- g_wannier: bfloat16 [512, 2, 512, 1024], P('row', None, None, 'blk'), may hold values from -0.03125 to 0.03125
- k_angle: float32 [256, 512], replicated, may hold values from -3.140625 to 3.140625
- q_angle: float32 [128, 512], replicated, may hold values from -3.140625 to 3.140625
- eig_k: bfloat16 [256, 2, 32, 32], P('row'), may hold values from -0.75 to 0.75
- eig_kq: bfloat16 [2048, 2, 32, 32], P(('row', 'blk')), may hold values from -0.75 to 0.75
- mask_k: int32 [256, 32], P('row'), may hold values 0 or 1
- mask_kq: int32 [2048, 32], P(('row', 'blk')), may hold values 0 or 1
- owner: int32 [4, 256, 32, 1], P('blk', 'row'), may hold values from 0 to 127; in each aligned block of 256 rows (0 to 255, 256 to 511, ..., all dimensions but the last counted through in order) at most 4 rows name the same one
- kq_local: int32 [4, 256, 32, 1], P('blk', 'row'), may hold values from 0 to 15
Outputs:
- couplings: bfloat16 [128, 256, 1024], P('blk', 'row')
Inputs may be any that keep to these rules, and one draw needn't show every extreme that they name: Within the pairs of one device (aligned blocks of 256 rows of the flattened leading dimensions) no owner is named more than 4 times, a bound that some block reaches.
All inputs are finite; a program needn't handle non-finite values. No bound on the sum of `mask_k` or of `mask_kq` on one device may be relied on, other than what follows from the above.
Results may differ from a plain program's by a relative error of at most 0.0073.
Values may be sent and summed in bfloat16 or wider, within the bound.
No kernel may reach another device: no remote copies, remote signals or barrier semaphores. Data moves between devices by JAX's collectives and lax.ppermute only.
A program may use at most 128 MiB of HBM per device.

v0:
```python
import jax
import jax.numpy as jnp
from jax import lax
from jax.sharding import PartitionSpec as P


def in_blocks(shard, dim, count):
    before, after = (shard.shape[:dim], shard.shape[dim + 1 :])
    return jnp.moveaxis(shard.reshape(*before, count, -1, *after), dim, 0)


def cut_rows(length, count):
    unit = 8 if length >= 8 * count else 1
    return [length // unit * k // count * unit for k in range(1, count)]


def laid_out(parts, dim):
    lengths = list(parts.shape[1:])
    lengths[dim] *= parts.shape[0]
    return jnp.moveaxis(parts, 0, dim).reshape(lengths)


def several_exchanges(shard, axis, pieces, split_dim, concat_dim):
    parts = in_blocks(shard, split_dim, lax.axis_size(axis))
    widest = max(range(1, max(2, parts.ndim - 1)), key=lambda d: parts.shape[d])
    done = []
    for slab in jnp.split(parts, cut_rows(parts.shape[widest], pieces), axis=widest):
        if slab.size:
            done.append(lax.all_to_all(slab, axis, split_axis=0, concat_axis=0, tiled=True))
    return laid_out(jnp.concatenate(done, axis=widest), concat_dim)


def rotate(vectors, halves):
    vec_real = vectors[:, 0]
    vec_imag = vectors[:, 1]
    half_real = halves[:, 0]
    half_imag = halves[:, 1]
    rot_real = jnp.einsum(
        "pim,pin->pmn", vec_real, half_real, preferred_element_type=jnp.float32
    ) + jnp.einsum("pim,pin->pmn", vec_imag, half_imag, preferred_element_type=jnp.float32)
    rot_imag = jnp.einsum(
        "pim,pin->pmn", vec_real, half_imag, preferred_element_type=jnp.float32
    ) - jnp.einsum("pim,pin->pmn", vec_imag, half_real, preferred_element_type=jnp.float32)
    squared = rot_real * rot_real + rot_imag * rot_imag
    return squared.astype(jnp.bfloat16).reshape(vectors.shape[0], -1)


def half_rotate(blocks, masked_k):
    half_real = jnp.einsum(
        "qkij,kjn->qkin", blocks[0], masked_k[:, 0], preferred_element_type=jnp.float32
    ) - jnp.einsum("qkij,kjn->qkin", blocks[1], masked_k[:, 1], preferred_element_type=jnp.float32)
    half_imag = jnp.einsum(
        "qkij,kjn->qkin", blocks[0], masked_k[:, 1], preferred_element_type=jnp.float32
    ) + jnp.einsum("qkij,kjn->qkin", blocks[1], masked_k[:, 0], preferred_element_type=jnp.float32)
    return jnp.stack([half_real, half_imag], 2).astype(jnp.bfloat16)


def shards(g_wannier, k_angle, q_angle, eig_k, eig_kq, mask_k, mask_kq, owner, kq_local):
    rp_local, _, re_count, e_local = g_wannier.shape
    k_all = k_angle.shape[0]
    q_all, rp_all = q_angle.shape
    k_local = eig_k.shape[0]
    band_count = eig_k.shape[2]
    row_count = lax.axis_size("row")
    blk_count = lax.axis_size("blk")
    devices = row_count * blk_count
    q_local = q_all // blk_count
    k_cos = jnp.cos(k_angle).astype(jnp.bfloat16)
    k_sin = jnp.sin(k_angle).astype(jnp.bfloat16)
    k_phase = jnp.concatenate(
        [jnp.concatenate([k_cos, -k_sin], 1), jnp.concatenate([k_sin, k_cos], 1)], 0
    )
    stacked = g_wannier.reshape(rp_local, 2 * re_count, e_local)
    k_part = jnp.einsum("ar,pre->pae", k_phase, stacked, preferred_element_type=jnp.float32)
    k_part = k_part.astype(jnp.bfloat16).reshape(rp_local, 2, k_all, e_local)
    regrouped = several_exchanges(k_part, "row", 2, 2, 0)
    q_cos = jnp.cos(q_angle).astype(jnp.bfloat16)
    q_sin = jnp.sin(q_angle).astype(jnp.bfloat16)
    q_phase = jnp.stack([jnp.stack([q_cos, -q_sin], 2), jnp.stack([q_sin, q_cos], 2)], 0).reshape(
        2 * q_all, 2 * rp_all
    )
    q_part = jnp.dot(
        q_phase,
        regrouped.reshape(2 * rp_all, k_local * e_local),
        preferred_element_type=jnp.float32,
    )
    q_part = q_part.astype(jnp.bfloat16).reshape(2, q_all, k_local, e_local)
    masked_k = eig_k * mask_k.astype(jnp.bfloat16)[:, None, None, :]
    masked_kq = eig_kq * mask_kq.astype(jnp.bfloat16)[:, None, None, :]
    pair_count = q_local * k_local
    capacity = max(2, 2 * pair_count // devices)
    owners = jnp.transpose(owner.reshape(k_local, q_local)).reshape(-1)
    local_ids = jnp.transpose(kq_local.reshape(k_local, q_local)).reshape(-1)
    matches = (owners[:, None] == jnp.arange(devices, dtype=jnp.int32)[None, :]).astype(jnp.int32)
    slot_rank = jnp.sum((jnp.cumsum(matches, 0) - matches) * matches, 1)
    position = owners * capacity + slot_rank
    coupling = lax.all_to_all(q_part, "blk", split_axis=1, concat_axis=3, tiled=True)
    blocks = coupling.reshape(2, q_local, k_local, band_count, band_count)
    half = half_rotate(blocks, masked_k).reshape(pair_count, 2, band_count * band_count)
    slot_ids = (
        jnp.zeros((devices * capacity,), jnp.int32)
        .at[position]
        .set(local_ids)
        .reshape(devices, capacity)
    )
    requested = lax.all_to_all(slot_ids, ("row", "blk"), split_axis=0, concat_axis=0, tiled=True)
    vectors = masked_kq[requested.reshape(-1)].reshape(
        devices, capacity, 2, band_count * band_count
    )
    fetched = lax.all_to_all(vectors, ("row", "blk"), split_axis=0, concat_axis=0, tiled=True)
    fetched_rows = fetched.reshape(devices * capacity, 2, band_count, band_count)[position]
    result = rotate(fetched_rows, half.reshape(pair_count, 2, band_count, band_count))
    return result.reshape(q_local, k_local, band_count * band_count)


def solution(mesh):
    placed = (
        P("row", None, None, "blk"),
        P(),
        P(),
        P("row", None, None, None),
        P(("row", "blk"), None, None, None),
        P("row", None),
        P(("row", "blk"), None),
        P("blk", "row", None, None),
        P("blk", "row", None, None),
    )
    return jax.shard_map(
        shards, mesh=mesh, in_specs=placed, out_specs=P("blk", "row", None), check_vma=False
    )
```

profile of v0, /device:TPU:1, one launch (start us, length us, event | category | flops | bytes accessed | tf_op | source)
XLA Modules:
  0.0 217.6 jit_solution(13129121934890681503)
XLA Ops:
  0.0 0.7 broadcast_multiply_fusion.2
  0.7 0.8 copy.27
  1.8 0.8 copy.31
  3.3 1.4 scatter_custom_fusion
  4.7 0.7 all_to_all.26
  5.4 11.5 %all-to-all-start = ((s32[128,1,4]{2,1,0:T(1,128)}), s32[128,1,4]{2,1,0:T(1,128)S(1)}, u32[]{:S(2)}, u32[]{:S(2)}) async-start(s32[128,1,4]{2,1,0:T(1,128)} %bitcast.10), calls=%async_computation | async-start | bytes 131072 | tf_op jit(solution)/shard_map/all_to_all | solution.py:106
  16.9 2.7 %cosine_convert_fusion = bf16[256,512]{1,0:T(8,128)(2,1)S(1)} fusion(f32[256,512]{1,0:T(8,128)} %param.10), kind=kLoop, calls=%fused_computation.29 | loop fusion | flops 131072 | bytes 786432 | tf_op jit(solution)/shard_map/convert_element_type | solution.py:68
  19.6 2.7 %fusion.25 = (bf16[256,512]{1,0:T(8,128)(2,1)S(1)}, bf16[256,512]{1,0:T(8,128)(2,1)S(1)}) fusion(f32[256,512]{1,0:T(8,128)} %param.10), kind=kLoop, calls=%fused_computation.61 | loop fusion | flops 524288 | bytes 1048576 | tf_op jit(solution)/shard_map/neg | solution.py:71
  22.3 11.3 %convolution_convert_fusion = bf16[512,16,256]{2,0,1:T(8,128)(2,1)S(1)} fusion(bf16[16,1024,256]{2,1,0:T(8,128)(2,1)} %bitcast.132, bf16[256,512]{1,0:T(8,128)(2,1)S(1)} %cosine_convert_fusion, bf16[256,512]{1,0:T(8,128)(2,1)S(1)} %get-tuple-element.6, bf16[256,512]{1,0:T(8,128)(2,1)S(1)} %get-tuple-element.5), kind=kOutput, calls=%fused_computation.8 | convolution fusion | flops 4301258752 | bytes 13369344 | tf_op jit(solution)/shard_map/ar,pre->pae/dot_general | solution.py:74
  33.6 0.5 copy.55
  34.1 1.7 fusion.26
  35.8 36.1 %all_to_all.39 = bf16[32,8,2,8,256]{4,3,2,1,0:T(8,128)(2,1)} all-to-all(bf16[32,8,2,8,256]{4,3,2,1,0:T(8,128)(2,1)S(1)} %get-tuple-element.7), channel_id=1, replica_groups=mesh['row'=32,'blk'=4] {'row'}, dimensions={0} | all-to-all | bytes 4194304 | tf_op jit(solution)/shard_map/all_to_all | solution.py:29
  71.9 4.1 %all-to-all-start.3 = ((bf16[32,8,2,8,256]{4,3,2,1,0:T(8,128)(2,1)}), bf16[32,8,2,8,256]{4,3,2,1,0:T(8,128)(2,1)S(1)}, u32[]{:S(2)}, u32[]{:S(2)}) async-start(bf16[32,8,2,8,256]{4,3,2,1,0:T(8,128)(2,1)} %get-tuple-element.8), calls=%async_computation.3 | async-start | bytes 4194304 | tf_op jit(solution)/shard_map/all_to_all | solution.py:29
  76.0 0.5 broadcast.88
  76.6 0.8 reduce.3
  77.5 13.4 %gather_fusion = bf16[512,2,32,32]{3,2,1,0:T(8,128)(2,1)} fusion(bf16[16,2,32,32]{3,2,1,0:T(8,128)(2,1)S(1)} %broadcast_multiply_fusion, s32[1024]{0:T(1024)S(1)} %pad_clamp_fusion.1), kind=kCustom, calls=%fused_computation | custom fusion | bytes 4196352 | tf_op jit(solution)/shard_map/gather | solution.py:107
  90.9 12.9 %reshape.127 = bf16[128,4,2,1024]{3,2,1,0:T(2,128)(2,1)} reshape(bf16[512,2,32,32]{3,2,1,0:T(8,128)(2,1)} %gather_fusion) | data formatting | bytes 4194304 | tf_op jit(solution)/shard_map/reshape | solution.py:107
  103.9 0.4 all-to-all-done.3
  104.2 1.3 copy-done.5
  105.6 9.1 %all-to-all-start.1 = ((bf16[128,4,2,1024]{3,2,1,0:T(2,128)(2,1)}), bf16[128,4,2,1024]{3,2,1,0:T(2,128)(2,1)S(1)}, u32[]{:S(2)}, u32[]{:S(2)}) async-start(bf16[128,4,2,1024]{3,2,1,0:T(2,128)(2,1)} %reshape.127), calls=%async_computation.1 | async-start | bytes 4194304 | tf_op jit(solution)/shard_map/all_to_all | solution.py:110
  114.7 0.9 negate_bitcast_fusion
  115.5 1.0 fusion.21
  116.6 0.4 copy.35
  117.0 2.6 %pad_maximum_fusion = bf16[32,16,2,8,256]{4,3,2,1,0:T(8,128)(2,1)S(1)} fusion(bf16[32,8,2,8,256]{4,3,2,1,0:T(8,128)(2,1)} %copy-done.5, bf16[32,8,2,8,256]{4,3,2,1,0:T(8,128)(2,1)} %all_to_all.39), kind=kLoop, calls=%fused_computation.3 | loop fusion | flops 2097152 | bytes 8388608 | tf_op jit(solution)/shard_map/concatenate | solution.py:30
  119.6 1.5 copy.47
  121.1 1.3 convolution_convert_fusion.1
  122.7 1.1 copy.37
  123.9 21.3 %all-to-all-done.1 = bf16[128,4,2,1024]{3,2,1,0:T(2,128)(2,1)S(1)} async-done(((bf16[128,4,2,1024]{3,2,1,0:T(2,128)(2,1)}), bf16[128,4,2,1024]{3,2,1,0:T(2,128)(2,1)S(1)}, u32[]{:S(2)}, u32[]{:S(2)}) %all-to-all-start.1) | async-done | bytes 2097184 | tf_op jit(solution)/shard_map/all_to_all | solution.py:110
  145.2 3.7 %all-to-all-start.4 = ((bf16[2,128,8,256]{3,2,0,1:T(8,128)(2,1)}), bf16[2,128,8,256]{3,2,0,1:T(8,128)(2,1)S(1)}, u32[]{:S(2)}, u32[]{:S(2)}) async-start(bf16[2,128,8,256]{3,2,0,1:T(8,128)(2,1)} %copy.37), calls=%async_computation.4 | async-start | bytes 2097152 | tf_op jit(solution)/shard_map/all_to_all | solution.py:97
  149.2 6.6 %reshape.128 = bf16[512,2,32,32]{3,2,1,0:T(8,128)(2,1)} reshape(bf16[128,4,2,1024]{3,2,1,0:T(2,128)(2,1)S(1)} %all-to-all-done.1) | data formatting | bytes 4194304 | tf_op jit(solution)/shard_map/reshape | solution.py:111
  155.8 6.4 %gather_fusion.1 = bf16[256,2,32,32]{3,2,1,0:T(8,128)(2,1)} fusion(bf16[512,2,32,32]{3,2,1,0:T(8,128)(2,1)} %reshape.128, s32[1024]{0:T(1024)S(1)} %pad_clamp_fusion), kind=kCustom, calls=%fused_computation.1 | custom fusion | bytes 2098176 | tf_op jit(solution)/shard_map/gather | solution.py:111
  162.2 1.4 all-to-all-done.4
  163.7 0.8 copy.56
  164.5 0.4 fusion.27
  164.9 0.9 squeeze.30
  165.8 5.2 %fusion.20 = f32[8,32,32,32]{3,1,2,0:T(8,128)} fusion(bf16[32,8,32,32]{3,2,0,1:T(8,128)(2,1)S(1)} %squeeze.30, bf16[8,2,32,32]{2,3,0,1:T(8,128)(2,1)S(1)} %broadcast_multiply_fusion.1), kind=kOutput, calls=%fused_computation.50 | convolution fusion | flops 16777216 | bytes 3211264 | tf_op jit(solution)/shard_map/qkij,kjn->qkin/dot_general | solution.py:52
  171.0 5.2 %fusion.19 = f32[8,32,32,32]{3,1,2,0:T(8,128)} fusion(bf16[32,8,32,32]{3,2,0,1:T(8,128)(2,1)S(1)} %squeeze.30, bf16[8,2,32,32]{2,3,0,1:T(8,128)(2,1)S(1)} %broadcast_multiply_fusion.1), kind=kOutput, calls=%fused_computation.49 | convolution fusion | flops 16777216 | bytes 3211264 | tf_op jit(solution)/shard_map/qkij,kjn->qkin/dot_general | solution.py:49
  176.2 0.9 squeeze.32
  177.1 6.8 %fusion.4 = bf16[32,8,32,32]{2,3,0,1:T(8,128)(2,1)} fusion(f32[8,32,32,32]{3,1,2,0:T(8,128)} %fusion.20, bf16[32,8,32,32]{3,2,0,1:T(8,128)(2,1)S(1)} %squeeze.32, bf16[8,2,32,32]{2,3,0,1:T(8,128)(2,1)S(1)} %broadcast_multiply_fusion.1), kind=kOutput, calls=%fused_computation.16 | convolution fusion | flops 17301504 | bytes 3735552 | tf_op jit(solution)/shard_map/qkij,kjn->qkin/dot_general | solution.py:54
  183.9 4.1 %copy.41 = bf16[32,8,32,32]{3,2,1,0:T(8,128)(2,1)} copy(bf16[32,8,32,32]{2,3,0,1:T(8,128)(2,1)} %fusion.4) | data formatting | bytes 1048576 | tf_op jit(solution)/shard_map/add | solution.py:52
  188.0 5.2 %fusion = f32[256,32,32]{2,1,0:T(8,128)} fusion(bf16[256,32,32]{2,1,0:T(8,128)(2,1)} %bitcast.111, bf16[256,2,32,32]{3,2,1,0:T(8,128)(2,1)} %gather_fusion.1), kind=kOutput, calls=%fused_computation.12 | convolution fusion | flops 16777216 | bytes 5242880 | tf_op jit(solution)/shard_map/pim,pin->pmn/dot_general | solution.py:41
  193.2 2.8 %fusion.2 = f32[256,32,32]{2,1,0:T(8,128)} fusion(bf16[256,32,32]{2,1,0:T(8,128)(2,1)S(1)} %bitcast.112, bf16[256,2,32,32]{3,2,1,0:T(8,128)(2,1)S(1)} %copy-done), kind=kOutput, calls=%fused_computation.14 | convolution fusion | flops 16777216 | bytes 5242880 | tf_op jit(solution)/shard_map/pim,pin->pmn/dot_general | solution.py:40
  196.3 4.6 %fusion.3 = bf16[32,8,32,32]{2,3,0,1:T(8,128)(2,1)} fusion(f32[8,32,32,32]{3,1,2,0:T(8,128)S(1)} %copy-done.3, bf16[32,8,32,32]{3,2,0,1:T(8,128)(2,1)S(1)} %squeeze.32, bf16[8,2,32,32]{2,3,0,1:T(8,128)(2,1)S(1)} %broadcast_multiply_fusion.1), kind=kOutput, calls=%fused_computation.15 | convolution fusion | flops 17301504 | bytes 6881280 | tf_op jit(solution)/shard_map/qkij,kjn->qkin/dot_general | solution.py:51
  200.9 3.5 %copy.39 = bf16[32,8,32,32]{3,2,1,0:T(8,128)(2,1)S(1)} copy(bf16[32,8,32,32]{2,3,0,1:T(8,128)(2,1)} %fusion.3) | data formatting | bytes 1048576 | tf_op jit(solution)/shard_map/sub | solution.py:49
  204.4 2.6 %fusion.1 = f32[256,32,32]{2,1,0:T(8,128)S(1)} fusion(bf16[256,32,32]{2,1,0:T(8,128)(2,1)S(1)} %bitcast.109, bf16[256,2,32,32]{3,2,1,0:T(8,128)(2,1)} %gather_fusion.1), kind=kOutput, calls=%fused_computation.13 | convolution fusion | flops 16777216 | bytes 3670016 | tf_op jit(solution)/shard_map/pim,pin->pmn/dot_general | solution.py:38
  207.2 1.3 copy-done.4
  208.5 4.9 %add_convert_fusion = bf16[256,32,32]{2,1,0:T(8,128)(2,1)} fusion(f32[256,32,32]{2,1,0:T(8,128)S(1)} %copy-done.4, f32[256,32,32]{2,1,0:T(8,128)S(1)} %fusion.1, f32[256,32,32]{2,1,0:T(8,128)} %fusion.2, bf16[256,32,32]{2,1,0:T(8,128)(2,1)S(1)} %bitcast.110, bf16[256,2,32,32]{3,2,1,0:T(8,128)(2,1)S(1)} %copy-done.1), kind=kOutput, calls=%fused_computation.5 | convolution fusion | flops 18350080 | bytes 14155776 | tf_op jit(solution)/shard_map/pim,pin->pmn/dot_general | solution.py:43
  213.3 4.2 %reshape_reshape.12 = bf16[32,8,1024]{2,1,0:T(8,128)(2,1)} reshape(bf16[256,32,32]{2,1,0:T(8,128)(2,1)} %add_convert_fusion) | data formatting | bytes 1048576 | tf_op jit(solution)/shard_map/reshape;reshape | solution.py:113
  (48 shorter events, 2.3 us)
Async XLA Ops:
  5.4 30.4 %all-to-all-start = ((s32[128,1,4]{2,1,0:T(1,128)}), s32[128,1,4]{2,1,0:T(1,128)S(1)}, u32[]{:S(2)}, u32[]{:S(2)}) async-start(s32[128,1,4]{2,1,0:T(1,128)} %bitcast.10), calls=%async_computation | async-start | bytes 131072 | tf_op jit(solution)/shard_map/all_to_all | solution.py:106
  35.8 40.2 %copy-start.9 = (s32[16,32]{1,0:T(8,128)S(1)}, s32[16,32]{1,0:T(8,128)}, u32[]{:S(2)}) copy-start(s32[16,32]{1,0:T(8,128)} %param.15) | copy-start | bytes 6148
  35.8 40.2 %copy-start.7 = (bf16[16,2,32,32]{3,2,1,0:T(8,128)(2,1)S(1)}, bf16[16,2,32,32]{3,2,1,0:T(8,128)(2,1)}, u32[]{:S(2)}) copy-start(bf16[16,2,32,32]{3,2,1,0:T(8,128)(2,1)} %param.13) | copy-start | bytes 196612
  71.9 32.3 %all-to-all-start.3 = ((bf16[32,8,2,8,256]{4,3,2,1,0:T(8,128)(2,1)}), bf16[32,8,2,8,256]{4,3,2,1,0:T(8,128)(2,1)S(1)}, u32[]{:S(2)}, u32[]{:S(2)}) async-start(bf16[32,8,2,8,256]{4,3,2,1,0:T(8,128)(2,1)} %get-tuple-element.8), calls=%async_computation.3 | async-start | bytes 4194304 | tf_op jit(solution)/shard_map/all_to_all | solution.py:29
  103.9 10.8 %copy-start.6 = (f32[128,512]{1,0:T(8,128)S(1)}, f32[128,512]{1,0:T(8,128)}, u32[]{:S(2)}) copy-start(f32[128,512]{1,0:T(8,128)} %param.11) | copy-start | bytes 786436
  104.2 1.3 copy-start.5
  105.6 39.6 %all-to-all-start.1 = ((bf16[128,4,2,1024]{3,2,1,0:T(2,128)(2,1)}), bf16[128,4,2,1024]{3,2,1,0:T(2,128)(2,1)S(1)}, u32[]{:S(2)}, u32[]{:S(2)}) async-start(bf16[128,4,2,1024]{3,2,1,0:T(2,128)(2,1)} %reshape.127), calls=%async_computation.1 | async-start | bytes 4194304 | tf_op jit(solution)/shard_map/all_to_all | solution.py:110
  122.4 26.5 %copy-start.10 = (s32[8,32]{1,0:T(8,128)S(1)}, s32[8,32]{1,0:T(8,128)}, u32[]{:S(2)}) copy-start(s32[8,32]{1,0:T(8,128)} %param.14) | copy-start | bytes 3076
  122.4 26.5 %copy-start.8 = (bf16[8,2,32,32]{3,2,1,0:T(8,128)(2,1)S(1)}, bf16[8,2,32,32]{3,2,1,0:T(8,128)(2,1)}, u32[]{:S(2)}) copy-start(bf16[8,2,32,32]{3,2,1,0:T(8,128)(2,1)} %param.12) | copy-start | bytes 98308
  145.2 18.5 %all-to-all-start.4 = ((bf16[2,128,8,256]{3,2,0,1:T(8,128)(2,1)}), bf16[2,128,8,256]{3,2,0,1:T(8,128)(2,1)S(1)}, u32[]{:S(2)}, u32[]{:S(2)}) async-start(bf16[2,128,8,256]{3,2,0,1:T(8,128)(2,1)} %copy.37), calls=%async_computation.4 | async-start | bytes 2097152 | tf_op jit(solution)/shard_map/all_to_all | solution.py:97
  188.0 5.2 %copy-start = (bf16[256,2,32,32]{3,2,1,0:T(8,128)(2,1)S(1)}, bf16[256,2,32,32]{3,2,1,0:T(8,128)(2,1)}, u32[]{:S(2)}) copy-start(bf16[256,2,32,32]{3,2,1,0:T(8,128)(2,1)} %gather_fusion.1) | copy-start | bytes 3145732
  188.0 5.2 %copy-start.2 = (bf16[32,8,32,32]{3,2,1,0:T(8,128)(2,1)S(1)}, bf16[32,8,32,32]{3,2,1,0:T(8,128)(2,1)}, u32[]{:S(2)}) copy-start(bf16[32,8,32,32]{3,2,1,0:T(8,128)(2,1)} %copy.41) | copy-start | bytes 1572868
  193.2 3.1 %copy-start.3 = (f32[8,32,32,32]{3,1,2,0:T(8,128)S(1)}, f32[8,32,32,32]{3,1,2,0:T(8,128)}, u32[]{:S(2)}) copy-start(f32[8,32,32,32]{3,1,2,0:T(8,128)} %fusion.19) | copy-start | bytes 3145732
  204.3 2.8 %copy-start.1 = (bf16[256,2,32,32]{3,2,1,0:T(8,128)(2,1)S(1)}, bf16[256,2,32,32]{3,2,1,0:T(8,128)(2,1)}, u32[]{:S(2)}) copy-start(bf16[256,2,32,32]{3,2,1,0:T(8,128)(2,1)} %gather_fusion.1) | copy-start | bytes 3145732
  204.4 4.1 %copy-start.4 = (f32[256,32,32]{2,1,0:T(8,128)S(1)}, f32[256,32,32]{2,1,0:T(8,128)}, u32[]{:S(2)}) copy-start(f32[256,32,32]{2,1,0:T(8,128)} %fusion) | copy-start | bytes 3145732
where the time goes:
time: 219 us; the launch traced here: 218 us
  local copies, waits for them, and re-layouts  67.8 us (31%)
  matrix products  49.8 us (23%)
  blocking collectives  36.1 us (16%)
  starting transfers between devices  28.4 us (13%)
  waiting for transfers between devices  23.1 us (11%)
  other arithmetic  11.9 us (5%)
    all_to_all x1, blocking collectives, several_exchanges(): lax.all_to_all(slab, axis, split_axis=0, concat_axis=0, tiled=True)  36.1 us
    all_to_all x1, waiting for transfers between devices, shards(): lax.all_to_all(vectors, ('row', 'blk'), split_axis=0, concat_axis=0, tile...  21.3 us
    gather x1, local copies, waits for them, and re-layouts, shards(): masked_kq[requested.reshape(-1)]  13.4 us
    reshape x1, local copies, waits for them, and re-layouts, shards(): masked_kq[requested.reshape(-1)]  12.9 us
    all_to_all x1, starting transfers between devices, shards(): lax.all_to_all(slot_ids, ('row', 'blk'), split_axis=0, concat_axis=0, til...  11.5 us
    dot_general x1, matrix products, shards(): jnp.einsum('ar,pre->pae', k_phase, stacked, preferred_element_type=jnp.fl...  11.3 us
    all_to_all x1, starting transfers between devices, shards(): lax.all_to_all(vectors, ('row', 'blk'), split_axis=0, concat_axis=0, tile...  9.1 us
    dot_general x1, matrix products, half_rotate(): jnp.einsum('qkij,kjn->qkin', blocks[1], masked_k[:, 0], preferred_element...  6.76 us
  transfers between devices with their start and end apart: 4, of which 3 were waited for; matrix products, arithmetic and copies ran while one was open for 32% of the time, Pallas kernels for 0%

commit v1 on v0

v1 whole, which is shorter than its diff:
```python
import jax
import jax.numpy as jnp
import numpy as np
from jax import lax
from jax.experimental import pallas as pl
from jax.experimental.pallas import tpu as pltpu
from jax.sharding import PartitionSpec as P


F32 = jnp.float32
BF16 = jnp.bfloat16
VMEM = pltpu.VMEM
SMEM = pltpu.SMEM


def fitted(fun, odd):
    top = 3.15**2
    nodes = 0.5 * top * (1 - np.cos(np.pi * (np.arange(64) + 0.5) / 64))
    root = np.sqrt(nodes)
    values = fun(root) / root if odd else fun(root)
    cheb = np.polynomial.chebyshev.Chebyshev.fit(nodes, values, 8, domain=[0, top])
    return [float(v) for v in cheb.convert(kind=np.polynomial.Polynomial).coef]


SIN_COEF = fitted(np.sin, True)
COS_COEF = fitted(np.cos, False)


def cos_sin(angle):
    square = angle * angle

    def horner(coef):
        total = jnp.full_like(square, coef[-1])
        for c in coef[-2::-1]:
            total = total * square + c
        return total

    return horner(COS_COEF), horner(SIN_COEF) * angle


def limit(mebibytes):
    return pltpu.CompilerParams(vmem_limit_bytes=mebibytes << 20)


def row_id(z, x, c):
    return ((z % 4) * 4 + x % 4) * 2 + c % 2


def row_shift(value, dz=0, dx=0, dc=0):
    pairs = [
        (row_id(z, x, c), row_id(z + dz, x + dx, c + dc))
        for z in range(4)
        for x in range(4)
        for c in range(2)
    ]
    return lax.ppermute(value, "row", pairs)


def blk_shift(value, dy):
    return lax.ppermute(value, "blk", [(y, (y + dy) % 4) for y in range(4)])


def k_phase_kernel(ang_ref, out_ref):
    cos, sin = cos_sin(ang_ref[...])
    cos = cos.astype(BF16)
    sin = sin.astype(BF16)
    out_ref[0:256, 0:512] = cos
    out_ref[0:256, 512:1024] = -sin
    out_ref[256:512, 0:512] = sin
    out_ref[256:512, 512:1024] = cos


def k_phase_of(k_angle):
    whole = pl.BlockSpec(memory_space=VMEM)
    return pl.pallas_call(
        k_phase_kernel,
        in_specs=[whole],
        out_specs=whole,
        out_shape=jax.ShapeDtypeStruct((512, 1024), BF16),
        cost_estimate=pl.CostEstimate(flops=1 << 23, bytes_accessed=2 << 20, transcendentals=0),
        compiler_params=limit(8),
        name="k_phase",
    )(k_angle)


def k_kernel(phase_ref, g_ref, out_ref, g_in, middle, packed, in_sems, out_sems):
    def load(rp):
        return pltpu.make_async_copy(g_ref.at[rp], g_in.at[rp], in_sems.at[rp])

    for rp in range(16):
        load(rp).start()

    def some(step, carry):
        for u in range(4):
            load(step * 4 + u).wait()
        for u in range(4):
            rp = step * 4 + u
            part = jnp.dot(
                phase_ref[...], g_in[rp].reshape(1024, 256), preferred_element_type=F32
            )
            middle[rp] = part.astype(BF16)
        return carry

    lax.fori_loop(0, 4, some, 0)

    def store(piece):
        at = pl.ds(piece * 4, 4)
        return pltpu.make_async_copy(packed.at[at], out_ref.at[at], out_sems.at[piece])

    for piece in range(8):
        for c in range(2):
            at = c * 256 + 32 * piece
            turned = jnp.swapaxes(middle[:, at : at + 32, :], 0, 1)
            packed[piece * 4 : piece * 4 + 4, c * 8 : c * 8 + 8] = turned.reshape(4, 8, 16, 256)
        store(piece).start()
    for piece in range(8):
        store(piece).wait()


def k_transform(phase, g):
    return pl.pallas_call(
        k_kernel,
        in_specs=[pl.BlockSpec(memory_space=VMEM), pl.BlockSpec(memory_space=pltpu.HBM)],
        out_specs=pl.BlockSpec(memory_space=pltpu.HBM),
        out_shape=jax.ShapeDtypeStruct((32, 16, 16, 256), BF16),
        scratch_shapes=[
            VMEM((16, 2, 512, 256), BF16),
            VMEM((16, 512, 256), BF16),
            VMEM((32, 16, 16, 256), BF16),
            pltpu.SemaphoreType.DMA((16,)),
            pltpu.SemaphoreType.DMA((8,)),
        ],
        cost_estimate=pl.CostEstimate(
            flops=2 * 16 * 512 * 1024 * 256, bytes_accessed=12 << 20, transcendentals=0
        ),
        compiler_params=limit(58),
        name="k_transform",
    )(phase, g)


def prep_kernel(me_ref, q_ref, eig_ref, mask_ref, phase_out, eig_out):
    b = me_ref[3]
    for bd in range(4):
        rows = pl.ds(pl.multiple_of(lax.rem(b + bd, 4) * 32, 32), 32)
        cos, sin = cos_sin(q_ref[rows, :])
        cos = cos.astype(BF16)
        sin = sin.astype(BF16)
        top = slice(bd * 32, bd * 32 + 32)
        low = slice(128 + bd * 32, 128 + bd * 32 + 32)
        phase_out[top, 0:512] = cos
        phase_out[top, 512:1024] = -sin
        phase_out[low, 0:512] = sin
        phase_out[low, 512:1024] = cos
    for k in range(8):
        mask = mask_ref[k : k + 1, :].astype(F32)
        er = eig_ref[k, 0].astype(F32) * mask
        ei = eig_ref[k, 1].astype(F32) * mask
        first = [er, ei, er, ei, ei, -er, ei, -er]
        second = [-ei, er, -ei, er, er, ei, er, ei]
        eig_out[k, 0:32] = jnp.concatenate(first, 1).astype(BF16)
        eig_out[k, 32:64] = jnp.concatenate(second, 1).astype(BF16)


def prep(me, q_angle, eig_k, mask_k):
    whole = pl.BlockSpec(memory_space=VMEM)
    return pl.pallas_call(
        prep_kernel,
        in_specs=[pl.BlockSpec(memory_space=SMEM), whole, whole, whole],
        out_specs=[whole, whole],
        out_shape=[
            jax.ShapeDtypeStruct((256, 1024), BF16),
            jax.ShapeDtypeStruct((8, 64, 256), BF16),
        ],
        cost_estimate=pl.CostEstimate(flops=1 << 22, bytes_accessed=1 << 20, transcendentals=0),
        compiler_params=limit(8),
        name="prep",
    )(me, q_angle, eig_k, mask_k)


def table_kernel(eig_ref, mask_ref, out_ref):
    for p in range(16):
        mask = mask_ref[p : p + 1, :].astype(F32)
        both = jnp.concatenate([eig_ref[p, 0], eig_ref[p, 1]], 0).astype(F32) * mask
        turned = jnp.transpose(both)
        out_ref[p] = jnp.concatenate([turned[0:16], turned[16:32]], 1).astype(BF16)


def table_of(eig_kq, mask_kq):
    whole = pl.BlockSpec(memory_space=VMEM)
    return pl.pallas_call(
        table_kernel,
        in_specs=[whole, whole],
        out_specs=whole,
        out_shape=jax.ShapeDtypeStruct((16, 16, 128), BF16),
        cost_estimate=pl.CostEstimate(flops=1 << 20, bytes_accessed=1 << 18, transcendentals=0),
        compiler_params=limit(8),
        name="table",
    )(eig_kq, mask_kq)


def pick_kernel(me_ref, idx_ref, *refs):
    parts, out_ref = refs[:10], refs[10]
    table, spread, sems = refs[11:]
    k = pl.program_id(0)

    @pl.when(k == 0)
    def _():
        copies = []
        for cd in range(2):
            own, y1, y3, y2a, y2b = parts[cd * 5 : cd * 5 + 5]
            at = cd * 1024
            for ref, start, size in (
                (own, at, 256),
                (y1, at + 256, 256),
                (y2a, at + 512, 128),
                (y2b, at + 640, 128),
                (y3, at + 768, 256),
            ):
                copies.append(
                    pltpu.make_async_copy(ref, table.at[pl.ds(start, size)], sems.at[len(copies)])
                )
        for copy in copies:
            copy.start()
        source = lax.broadcasted_iota(jnp.int32, (128, 1024), 0)
        target = lax.broadcasted_iota(jnp.int32, (128, 1024), 1) // 8
        wanted = (target // 32) * 32 + (target + 8 * me_ref[3]) % 32
        spread[...] = jnp.where(source == wanted, 1.0, 0.0).astype(BF16)
        for copy in copies:
            copy.wait()

    row = lax.broadcasted_iota(jnp.int32, (128, 512), 0)
    lane = lax.broadcasted_iota(jnp.int32, (128, 512), 1)
    same = row % 8 == lane % 8
    groups = []
    for group in range(4):
        tiles = jnp.stack([table[idx_ref[k, group * 8 + u]].astype(F32) for u in range(8)])
        groups.append(jnp.swapaxes(tiles, 0, 1).reshape(128, 128).astype(BF16))
    tiles = jnp.concatenate(groups, 0)
    for h in range(2):
        at = slice(h * 512, h * 512 + 512)
        wide = jnp.dot(tiles, spread[:, at], preferred_element_type=F32)
        for group in range(4):
            kept = jnp.where(same, wide[group * 128 : group * 128 + 128], 0.0)
            out_ref[group, h * 128 : h * 128 + 128] = kept.astype(BF16)


def pick(me, idx, parts):
    return pl.pallas_call(
        pick_kernel,
        grid=(8,),
        in_specs=[pl.BlockSpec(memory_space=SMEM)] * 2 + [pl.BlockSpec(memory_space=pl.ANY)] * 10,
        out_specs=pl.BlockSpec((None, 4, 256, 512), lambda k: (k, 0, 0, 0)),
        out_shape=jax.ShapeDtypeStruct((8, 4, 256, 512), BF16),
        scratch_shapes=[
            VMEM((2048, 16, 128), BF16),
            VMEM((128, 1024), BF16),
            pltpu.SemaphoreType.DMA((10,)),
        ],
        cost_estimate=pl.CostEstimate(
            flops=2 * 32 * 128 * 128 * 1024, bytes_accessed=18 << 20, transcendentals=0
        ),
        compiler_params=limit(16),
        name="pick",
    )(me, idx, *parts)


def q_kernel(phase_ref, data_ref, o0, o1, o2, o3, data, sems):
    outs = (o0, o1, o2, o3)

    def load(k, part):
        return pltpu.make_async_copy(
            data_ref.at[:, part * 8 + k], data.at[k, part], sems.at[k, part]
        )

    for k in range(8):
        for part in range(2):
            load(k, part).start()
    for first in (0, 4):
        for k in range(first, first + 4):
            for part in range(2):
                load(k, part).wait()
        for k in range(first, first + 4):
            stacked = data[k].reshape(1024, 256)
            result = jnp.dot(phase_ref[...], stacked, preferred_element_type=F32).astype(BF16)
            for part in range(2):
                for bd in range(4):
                    at = (part * 4 + bd) * 32
                    outs[bd][k, part] = result[at : at + 32]


def q_transform(phase, data):
    whole = pl.BlockSpec(memory_space=VMEM)
    return pl.pallas_call(
        q_kernel,
        in_specs=[whole, pl.BlockSpec(memory_space=pl.ANY)],
        out_specs=[whole] * 4,
        out_shape=[jax.ShapeDtypeStruct((8, 2, 32, 256), BF16)] * 4,
        scratch_shapes=[
            VMEM((8, 2, 32, 16, 256), BF16),
            pltpu.SemaphoreType.DMA((8, 2)),
        ],
        cost_estimate=pl.CostEstimate(
            flops=2 * 8 * 256 * 1024 * 256, bytes_accessed=6 << 20, transcendentals=0
        ),
        compiler_params=limit(12),
        name="q_transform",
    )(phase, data)


def rotate_kernel(eig_ref, w_ref, a0, a1, a2, a3, out_ref, even, odd, merged, done):
    arrays = (a0, a1, a2, a3)
    quarter = lax.broadcasted_iota(jnp.int32, (8, 128), 1) // 32

    def first(k, halves):
        columns = []
        for part in range(2):
            whole = jnp.concatenate([ref[k, part] for ref in arrays], 0)
            columns.append((whole[:, 0:128], whole[:, 128:256]))
        both = jnp.concatenate(
            [jnp.concatenate([columns[0][hi], columns[1][hi]], 1) for hi in range(2)], 0
        )
        for low in range(4):
            blocks = []
            for part in range(2):
                for at in range(4):
                    block = eig_ref[k, part * 32 : part * 32 + 32]
                    blocks.append(block if at == low else jnp.zeros_like(block))
            half = jnp.dot(both, jnp.concatenate(blocks, 0), preferred_element_type=F32)
            for hi in range(2):
                for bd in range(4):
                    for group in range(4):
                        at = hi * 128 + bd * 32 + group * 8
                        place = (bd * 8 + hi * 4 + low) * 8
                        halves[group, place : place + 8] = half[at : at + 8, 0:128]
                        halves[group, 256 + place : 264 + place] = half[at : at + 8, 128:256]

    def second(k, halves):
        for group in range(4):
            rotated = jnp.dot(
                w_ref[k, group], halves[group].astype(BF16), preferred_element_type=F32
            )
            square = rotated * rotated
            square = square + pltpu.roll(square, 32, 1)
            for m in range(8):
                parts = [square[(4 * m + mm) * 8 : (4 * m + mm) * 8 + 8] for mm in range(4)]
                merged[group * 8 : group * 8 + 8, m * 128 : m * 128 + 128] = jnp.where(
                    quarter == 0,
                    parts[0],
                    jnp.where(
                        quarter == 1, parts[1], jnp.where(quarter == 2, parts[2], parts[3])
                    ),
                )
        done[k] = merged[...].astype(BF16)

    first(0, even)

    def two(step, carry):
        first(2 * step + 1, odd)
        second(2 * step, even)
        first(2 * step + 2, even)
        second(2 * step + 1, odd)
        return carry

    lax.fori_loop(0, 3, two, 0)
    first(7, odd)
    second(6, even)
    second(7, odd)
    out_ref[...] = jnp.swapaxes(done[...], 0, 1)


def rotate(eig, picked, arrays):
    whole = pl.BlockSpec(memory_space=VMEM)
    return pl.pallas_call(
        rotate_kernel,
        in_specs=[whole] * 6,
        out_specs=whole,
        out_shape=jax.ShapeDtypeStruct((32, 8, 1024), BF16),
        scratch_shapes=[
            VMEM((4, 512, 128), F32),
            VMEM((4, 512, 128), F32),
            VMEM((32, 1024), F32),
            VMEM((8, 32, 1024), BF16),
        ],
        cost_estimate=pl.CostEstimate(
            flops=2 * 8 * 4 * (256 * 256 * 256 + 256 * 512 * 128),
            bytes_accessed=12 << 20,
            transcendentals=0,
        ),
        compiler_params=limit(12),
        name="rotate",
    )(eig, picked, *arrays)


def shards(g_wannier, k_angle, q_angle, eig_k, eig_kq, mask_k, mask_kq, owner, kq_local):
    row = lax.axis_index("row")
    b = lax.axis_index("blk")
    z, x, c = row // 8, (row // 2) % 4, row % 2
    me = jnp.stack([z, x, c, b]).astype(jnp.int32)

    table = table_of(eig_kq, mask_kq)
    table, k_angle = lax.optimization_barrier((table, k_angle))
    from_x = []
    for d in (1, 2, 3):
        from_x.append(row_shift(table, dx=-d))
    along_x = jnp.stack([table] + from_x)
    from_z = []
    for d in (1, 2, 3):
        from_z.append(row_shift(along_x, dz=-d))
    along_z = jnp.stack([along_x] + from_z)
    y1 = blk_shift(along_z, -1)
    y3 = blk_shift(along_z, 1)
    y2a = blk_shift(y1[0:2], -1)
    y2b = blk_shift(y3[2:4], 1)
    own = [along_z, y1, y3, y2a, y2b]
    other = [row_shift(part, dc=1) for part in own]
    parts = [part.reshape(-1, 16, 128) for part in own + other]

    own_row = owner.reshape(8, 32) // 4
    c_off = (own_row - c) % 2
    y_off = (owner.reshape(8, 32) - b) % 4
    z_off = (own_row // 8 - z) % 4
    x_off = (own_row // 2 - x) % 4
    idx = (((c_off * 4 + y_off) * 4 + z_off) * 4 + x_off) * 16 + kq_local.reshape(8, 32)

    k_phase = k_phase_of(k_angle)
    sent = k_transform(k_phase, g_wannier)
    taken = lax.all_to_all(sent, "row", split_axis=0, concat_axis=0, tiled=True)

    phase, eig = prep(me, q_angle, eig_k, mask_k)
    picked = pick(me, idx, parts)
    outs = q_transform(phase, taken)
    arrays = {0: outs[0]}
    for d in (1, 2, 3):
        arrays[(-d) % 4] = blk_shift(outs[d], d)
    return rotate(eig, picked, [arrays[off] for off in range(4)])


def solution(mesh):
    placed = (
        P("row", None, None, "blk"),
        P(),
        P(),
        P("row", None, None, None),
        P(("row", "blk"), None, None, None),
        P("row", None),
        P(("row", "blk"), None),
        P("blk", "row", None, None),
        P("blk", "row", None, None),
    )

    return jax.shard_map(
        shards, mesh=mesh, in_specs=placed, out_specs=P("blk", "row", None), check_vma=False
    )
```

time: 219 us -> 168 us (0.77)
  waiting for transfers between devices: 23.1 us -> 97 us
  local copies, waits for them, and re-layouts: 67.8 us -> 6.59 us
  matrix products: 49.8 us -> 0 us
  blocking collectives: 36.1 us -> 0 us
  Pallas kernels: 0 us -> 27.6 us
  other arithmetic: 11.9 us -> 0.29 us
  starting transfers between devices: 28.4 us -> 35.4 us
    ppermute x0 -> x18, waiting for transfers between devices: none -> 97 us  [the longest x11 59.6 us: row_shift(): return lax.ppermute(value, 'row', pairs)]
    dot_general x10 -> x0, matrix products: 49.8 us -> none  [the longest x1 11.3 us: shards(): jnp.einsum('ar,pre->pae', k_phase, stacked, preferred_element_type=jnp.fl...]
    all_to_all x1 -> x0, blocking collectives: 36.1 us -> none  [several_exchanges(): lax.all_to_all(slab, axis, split_axis=0, concat_axis=0, tiled=True)]
    pallas_call x0 -> x7, Pallas kernels: none -> 27.6 us  [the longest x1 10.1 us: k_transform(): pl.pallas_call(k_kernel, in_specs=[pl.BlockSpec(memory_space=VMEM), pl.Bl...]
    ppermute x0 -> x18, starting transfers between devices: none -> 25.8 us  [the longest x11 19.3 us: row_shift(): return lax.ppermute(value, 'row', pairs)]
    all_to_all x4 -> x1, waiting for transfers between devices: 23.1 us -> 0.01 us  [shards(): taken = lax.all_to_all(sent, 'row', split_axis=0, concat_axis=0, tiled=True)]
    reshape x5 -> x0, local copies, waits for them, and re-layouts: 20.8 us -> none  [the longest x1 12.9 us: shards(): masked_kq[requested.reshape(-1)]]
    gather x2 -> x0, local copies, waits for them, and re-layouts: 19.9 us -> none  [the longest x1 13.4 us: shards(): masked_kq[requested.reshape(-1)]]
  transfers between devices with their start and end apart: 4 -> 19, of which waited for: 3 -> 8; matrix products, arithmetic and copies ran while one was open for 32% -> 0% of each run, Pallas kernels for 0% -> 7%
where the time goes in v1:
time: 168 us; the launch traced here: 167 us
  waiting for transfers between devices  97 us (58%)
  starting transfers between devices  35.4 us (21%)
  Pallas kernels  27.6 us (16%)
  local copies, waits for them, and re-layouts  6.59 us (4%)
    ppermute x11, waiting for transfers between devices, row_shift(): return lax.ppermute(value, 'row', pairs)  59.6 us
    ppermute x7, waiting for transfers between devices, blk_shift(): return lax.ppermute(value, 'blk', [(y, (y + dy) % 4) for y in range(4)])  37.4 us
    ppermute x11, starting transfers between devices, row_shift(): return lax.ppermute(value, 'row', pairs)  19.3 us
    pallas_call x1, Pallas kernels, k_transform(): pl.pallas_call(k_kernel, in_specs=[pl.BlockSpec(memory_space=VMEM), pl.Bl...  10.1 us
    all_to_all x1, starting transfers between devices, shards(): taken = lax.all_to_all(sent, 'row', split_axis=0, concat_axis=0, tiled=True)  9.62 us
    pallas_call x1, Pallas kernels, pick(): pl.pallas_call(pick_kernel, grid=(8,), in_specs=[pl.BlockSpec(memory_spac...  6.96 us
    unnamed x22, local copies, waits for them, and re-layouts  6.52 us
    ppermute x7, starting transfers between devices, blk_shift(): return lax.ppermute(value, 'blk', [(y, (y + dy) % 4) for y in range(4)])  6.48 us
  transfers between devices with their start and end apart: 19, of which 8 were waited for; matrix products, arithmetic and copies ran while one was open for 0% of the time, Pallas kernels for 7%

profile of v1, /device:TPU:1, one launch (start us, length us, event | category | flops | bytes accessed | tf_op | source)
XLA Modules:
  0.0 167.1 jit_solution(2888529480116393720)
XLA Ops:
  0.0 0.9 copy-done.5
  1.0 0.7 copy-done.7
  1.6 0.3 table.1
  1.9 1.0 copy-done.1
  3.0 0.6 k_phase.1.phase_ref
  3.6 1.0 copy-done
  4.7 10.1 %k_transform.1 = bf16[32,16,16,256]{3,2,1,0:T(8,128)(2,1)} custom-call(bf16[512,1024]{1,0:T(8,128)(2,1)} %copy-done, bf16[16,2,512,256]{3,2,1,0:T(8,128)(2,1)} %g_ref.1), custom_call_target="tpu_custom_call" | custom-call | flops 4294967296 | bytes 12582912 | tf_op jit(solution)/shard_map/k_transform/pallas_call | solution.py:121
  14.8 0.0 copy-start.6
  14.8 0.0 copy-start.8
  14.8 0.0 copy-start.9
  14.8 0.0 copy-start.10
  14.8 9.6 %all-to-all-start = ((bf16[32,16,16,256]{3,2,1,0:T(8,128)(2,1)}), bf16[32,16,16,256]{3,2,1,0:T(8,128)(2,1)}, u32[]{:S(2)}, u32[]{:S(2)}) async-start(bf16[32,16,16,256]{3,2,1,0:T(8,128)(2,1)} %k_transform.1), calls=%async_computation | async-start | bytes 8388608 | tf_op jit(solution)/shard_map/all_to_all | solution.py:427
  24.5 1.4 collective-permute-start.2
  25.9 2.4 %collective-permute-start.1 = (bf16[16,16,128]{2,1,0:T(8,128)(2,1)S(1)}, bf16[16,16,128]{2,1,0:T(8,128)(2,1)S(1)}, u32[]{:S(2)}, u32[]{:S(2)}) collective-permute-start(bf16[16,16,128]{2,1,0:T(8,128)(2,1)S(1)} %table.1), channel_id=1, source_target_pairs={{0,16},{4,20},{8,24},{12,28},{16,0},{20,4},{24,8},{28,12},{32,48},... | collective-permute-start | bytes 196616 | tf_op jit(solution)/shard_map/ppermute | solution.py:56
  28.3 1.2 collective-permute-start
  29.5 44.7 %collective-permute-done.2 = bf16[16,16,128]{2,1,0:T(8,128)(2,1)S(1)} collective-permute-done((bf16[16,16,128]{2,1,0:T(8,128)(2,1)S(1)}, bf16[16,16,128]{2,1,0:T(8,128)(2,1)S(1)}, u32[]{:S(2)}, u32[]{:S(2)}) %collective-permute-start.2) | collective-permute-done | bytes 65568 | tf_op jit(solution)/shard_map/ppermute | solution.py:56
  74.2 4.3 %collective-permute-done.1 = bf16[16,16,128]{2,1,0:T(8,128)(2,1)S(1)} collective-permute-done((bf16[16,16,128]{2,1,0:T(8,128)(2,1)S(1)}, bf16[16,16,128]{2,1,0:T(8,128)(2,1)S(1)}, u32[]{:S(2)}, u32[]{:S(2)}) %collective-permute-start.1) | collective-permute-done | bytes 65568 | tf_op jit(solution)/shard_map/ppermute | solution.py:56
  78.5 1.5 collective-permute-start.5
  80.0 2.5 %collective-permute-start.4 = (bf16[4,16,16,128]{3,2,1,0:T(8,128)(2,1)S(1)}, bf16[4,16,16,128]{3,2,1,0:T(8,128)(2,1)S(1)}, u32[]{:S(2)}, u32[]{:S(2)}) collective-permute-start(bf16[4,16,16,128]{3,2,1,0:T(8,128)(2,1)S(1)} %get-tuple-element.22), channel_id=1, source_target_pairs={{0,64},{4,68},{8,72},{12,76},{16,80},{20,84},{24,88},{28,92},{32,9... | collective-permute-start | bytes 786440 | tf_op jit(solution)/shard_map/ppermute | solution.py:56
  82.4 0.5 collective-permute-start.3
  82.9 3.8 %collective-permute-done.5 = bf16[4,16,16,128]{3,2,1,0:T(8,128)(2,1)S(1)} collective-permute-done((bf16[4,16,16,128]{3,2,1,0:T(8,128)(2,1)S(1)}, bf16[4,16,16,128]{3,2,1,0:T(8,128)(2,1)S(1)}, u32[]{:S(2)}, u32[]{:S(2)}) %collective-permute-start.5) | collective-permute-done | bytes 262176 | tf_op jit(solution)/shard_map/ppermute | solution.py:56
  86.7 6.8 %collective-permute-done.4 = bf16[4,16,16,128]{3,2,1,0:T(8,128)(2,1)S(1)} collective-permute-done((bf16[4,16,16,128]{3,2,1,0:T(8,128)(2,1)S(1)}, bf16[4,16,16,128]{3,2,1,0:T(8,128)(2,1)S(1)}, u32[]{:S(2)}, u32[]{:S(2)}) %collective-permute-start.4) | collective-permute-done | bytes 262176 | tf_op jit(solution)/shard_map/ppermute | solution.py:56
  93.5 0.0 collective-permute-done.3
  93.5 0.1 pad_maximum_fusion
  93.6 2.8 %collective-permute-start.6 = (bf16[4,4,16,16,128]{4,3,2,1,0:T(8,128)(2,1)S(1)}, bf16[4,4,16,16,128]{4,3,2,1,0:T(8,128)(2,1)S(1)}, u32[]{:S(2)}, u32[]{:S(2)}) collective-permute-start(bf16[4,4,16,16,128]{4,3,2,1,0:T(8,128)(2,1)S(1)} %pad_maximum_fusion), channel_id=1, source_target_pairs={{0,3},{1,0},{2,1},{3,2},{4,7},{5,4},{6,5},{7,6},{8,11},{9,8},{10,9... | collective-permute-start | bytes 3145736 | tf_op jit(solution)/shard_map/ppermute | solution.py:60
  96.4 2.1 %collective-permute-start.10 = (bf16[4,4,16,16,128]{4,3,2,1,0:T(8,128)(2,1)S(1)}, bf16[4,4,16,16,128]{4,3,2,1,0:T(8,128)(2,1)}, u32[]{:S(2)}, u32[]{:S(2)}) collective-permute-start(bf16[4,4,16,16,128]{4,3,2,1,0:T(8,128)(2,1)S(1)} %pad_maximum_fusion), channel_id=1, source_target_pairs={{0,4},{4,0},{8,12},{12,8},{16,20},{20,16},{24,28},{28,24},{32,36},... | collective-permute-start | bytes 3145736 | tf_op jit(solution)/shard_map/ppermute | solution.py:56
  98.5 18.6 %collective-permute-done.6 = bf16[4,4,16,16,128]{4,3,2,1,0:T(8,128)(2,1)S(1)} collective-permute-done((bf16[4,4,16,16,128]{4,3,2,1,0:T(8,128)(2,1)S(1)}, bf16[4,4,16,16,128]{4,3,2,1,0:T(8,128)(2,1)S(1)}, u32[]{:S(2)}, u32[]{:S(2)}) %collective-permute-start.6) | collective-permute-done | bytes 1048608 | tf_op jit(solution)/shard_map/ppermute | solution.py:60
  117.1 2.7 %collective-permute-start.11 = (bf16[4,4,16,16,128]{4,3,2,1,0:T(8,128)(2,1)S(1)}, bf16[4,4,16,16,128]{4,3,2,1,0:T(8,128)(2,1)}, u32[]{:S(2)}, u32[]{:S(2)}) collective-permute-start(bf16[4,4,16,16,128]{4,3,2,1,0:T(8,128)(2,1)S(1)} %collective-permute-done.6), channel_id=1, source_target_pairs={{0,4},{4,0},{8,12},{12,8},{16,20},{20,16},{24,28},{28,24},{32,36},... | collective-permute-start | bytes 3145736 | tf_op jit(solution)/shard_map/ppermute | solution.py:56
  119.8 0.5 collective-permute-done.7
  120.3 3.0 %collective-permute-start.12 = (bf16[4,4,16,16,128]{4,3,2,1,0:T(8,128)(2,1)S(1)}, bf16[4,4,16,16,128]{4,3,2,1,0:T(8,128)(2,1)}, u32[]{:S(2)}, u32[]{:S(2)}) collective-permute-start(bf16[4,4,16,16,128]{4,3,2,1,0:T(8,128)(2,1)S(1)} %collective-permute-done.7), channel_id=1, source_target_pairs={{0,4},{4,0},{8,12},{12,8},{16,20},{20,16},{24,28},{28,24},{32,36},... | collective-permute-start | bytes 3145736 | tf_op jit(solution)/shard_map/ppermute | solution.py:56
  123.3 0.1 collective-permute-start.8
  123.4 1.5 collective-permute-start.9
  124.9 12.0 %collective-permute-done.8 = bf16[2,4,16,16,128]{4,3,2,1,0:T(8,128)(2,1)} collective-permute-done((bf16[2,4,16,16,128]{4,3,2,1,0:T(8,128)(2,1)S(1)}, bf16[2,4,16,16,128]{4,3,2,1,0:T(8,128)(2,1)}, u32[]{:S(2)}, u32[]{:S(2)}) %collective-permute-start.8) | collective-permute-done | bytes 524320 | tf_op jit(solution)/shard_map/ppermute | solution.py:60
  136.9 0.9 collective-permute-start.13
  137.8 1.3 collective-permute-start.14
  139.1 0.1 pad_add_fusion.me_ref
  139.2 0.9 copy-done.4
  140.2 1.0 prep.1
  141.2 0.0 copy-start.2
  141.2 0.8 copy-done.2
  142.0 1.0 copy-done.3
  143.0 3.1 %q_transform.1 = (bf16[8,2,32,256]{3,2,1,0:T(8,128)(2,1)S(1)}, bf16[8,2,32,256]{3,2,1,0:T(8,128)(2,1)S(1)}, bf16[8,2,32,256]{3,2,1,0:T(8,128)(2,1)S(1)}, bf16[8,2,32,256]{3,2,1,0:T(8,128)(2,1)S(1)}) custom-call(bf16[256,1024]{1,0:T(8,128)(2,1)S(1)} %copy-done.3, bf16[32,16,16,256]{3,2,1,0:T(8,128)(2,1)} %all-to-all-done.data_ref), custom_call_target="tpu_custom_call" | custom-call | flops 1073741824 | bytes 6291456 | tf_op jit(solution)/shard_map/q_transform/pallas_call | solution.py:293
  146.2 0.1 collective-permute-start.15
  146.3 2.0 %collective-permute-start.16 = (bf16[8,2,32,256]{3,2,1,0:T(8,128)(2,1)S(1)}, bf16[8,2,32,256]{3,2,1,0:T(8,128)(2,1)S(1)}, u32[]{:S(2)}, u32[]{:S(2)}) collective-permute-start(bf16[8,2,32,256]{3,2,1,0:T(8,128)(2,1)S(1)} %get-tuple-element.19), channel_id=1, source_target_pairs={{0,2},{1,3},{2,0},{3,1},{4,6},{5,7},{6,4},{7,5},{8,10},{9,11},{10,... | collective-permute-start | bytes 786440 | tf_op jit(solution)/shard_map/ppermute | solution.py:60
  148.3 0.0 collective-permute-start.17
  148.4 7.0 %pick.1.w_ref = bf16[8,4,256,512]{3,2,1,0:T(8,128)(2,1)S(1)} custom-call(s32[4]{0:T(128)S(1)} %pad_add_fusion.me_ref, s32[8,32]{1,0:T(8,128)S(1)} %fusion.9.idx_ref, bf16[256,16,128]{2,1,0:T(8,128)(2,1)S(1)} %bitcast.25, bf16[256,16,128]{2,1,0:T(8,128)(2,1)S(1)} %bitcast.26, bf16[256,16,128]{2,1,0:T(8,128)(2,1)S(1)} %bitcast.27, ...), custom_call_target="tpu_custom_call" | custom-call | flops 1073741824 | bytes 18874368 | tf_op jit(solution)/shard_map/pick/pallas_call | solution.py:248
  155.3 6.4 %collective-permute-done.17.a3 = bf16[8,2,32,256]{3,2,1,0:T(8,128)(2,1)S(1)} collective-permute-done((bf16[8,2,32,256]{3,2,1,0:T(8,128)(2,1)S(1)}, bf16[8,2,32,256]{3,2,1,0:T(8,128)(2,1)S(1)}, u32[]{:S(2)}, u32[]{:S(2)}) %collective-permute-start.17) | collective-permute-done | bytes 262176 | tf_op jit(solution)/shard_map/ppermute | solution.py:60
  161.7 5.4 %rotate.1 = bf16[32,8,1024]{2,1,0:T(8,128)(2,1)} custom-call(bf16[8,64,256]{2,1,0:T(8,128)(2,1)S(1)} %get-tuple-element.13.eig_ref, bf16[8,4,256,512]{3,2,1,0:T(8,128)(2,1)S(1)} %pick.1.w_ref, bf16[8,2,32,256]{3,2,1,0:T(8,128)(2,1)S(1)} %get-tuple-element.17.a0, bf16[8,2,32,256]{3,2,1,0:T(8,128)(2,1)S(1)} %collective-permute-done.15.a1, ...), custom_call_target="tpu_custom_call" | custom-call | flops 2147483648 | bytes 12582912 | tf_op jit(solution)/shard_map/rotate/pallas_call | solution.py:373
  (25 shorter events, 0.2 us)
Async XLA Ops:
  0.0 0.9 copy-start.5
  1.0 0.7 copy-start.7
  1.9 1.0 copy-start.1
  3.6 1.0 copy-start
  14.8 124.4 %copy-start.6 = (bf16[8,2,32,32]{3,2,1,0:T(8,128)(2,1)S(1)}, bf16[8,2,32,32]{3,2,1,0:T(8,128)(2,1)}, u32[]{:S(2)}) copy-start(bf16[8,2,32,32]{3,2,1,0:T(8,128)(2,1)} %eig_ref.2) | copy-start | bytes 98308
  14.8 124.4 %copy-start.8 = (s32[8,32]{1,0:T(8,128)S(1)}, s32[8,32]{1,0:T(8,128)}, u32[]{:S(2)}) copy-start(s32[8,32]{1,0:T(8,128)} %mask_ref.2) | copy-start | bytes 3076
  14.8 133.5 %copy-start.9 = (s32[1,8,32,1]{2,3,1,0:T(1,128)S(1)}, s32[1,8,32,1]{2,3,1,0:T(1,128)}, u32[]{:S(2)}) copy-start(s32[1,8,32,1]{2,3,1,0:T(1,128)} %param.17) | copy-start | bytes 3076
  14.8 133.5 %copy-start.10 = (s32[1,8,32,1]{2,3,1,0:T(1,128)S(1)}, s32[1,8,32,1]{2,3,1,0:T(1,128)}, u32[]{:S(2)}) copy-start(s32[1,8,32,1]{2,3,1,0:T(1,128)} %param.16) | copy-start | bytes 3076
  14.8 127.2 %all-to-all-start = ((bf16[32,16,16,256]{3,2,1,0:T(8,128)(2,1)}), bf16[32,16,16,256]{3,2,1,0:T(8,128)(2,1)}, u32[]{:S(2)}, u32[]{:S(2)}) async-start(bf16[32,16,16,256]{3,2,1,0:T(8,128)(2,1)} %k_transform.1), calls=%async_computation | async-start | bytes 8388608 | tf_op jit(solution)/shard_map/all_to_all | solution.py:427
  24.5 49.7 %collective-permute-start.2 = (bf16[16,16,128]{2,1,0:T(8,128)(2,1)S(1)}, bf16[16,16,128]{2,1,0:T(8,128)(2,1)S(1)}, u32[]{:S(2)}, u32[]{:S(2)}) collective-permute-start(bf16[16,16,128]{2,1,0:T(8,128)(2,1)S(1)} %table.1), channel_id=1, source_target_pairs={{0,8},{4,12},{8,16},{12,20},{16,24},{20,28},{24,0},{28,4},{32,40},... | collective-permute-start | bytes 196616 | tf_op jit(solution)/shard_map/ppermute | solution.py:56
  25.9 52.6 %collective-permute-start.1 = (bf16[16,16,128]{2,1,0:T(8,128)(2,1)S(1)}, bf16[16,16,128]{2,1,0:T(8,128)(2,1)S(1)}, u32[]{:S(2)}, u32[]{:S(2)}) collective-permute-start(bf16[16,16,128]{2,1,0:T(8,128)(2,1)S(1)} %table.1), channel_id=1, source_target_pairs={{0,16},{4,20},{8,24},{12,28},{16,0},{20,4},{24,8},{28,12},{32,48},... | collective-permute-start | bytes 196616 | tf_op jit(solution)/shard_map/ppermute | solution.py:56
  28.3 50.2 %collective-permute-start = (bf16[16,16,128]{2,1,0:T(8,128)(2,1)S(1)}, bf16[16,16,128]{2,1,0:T(8,128)(2,1)S(1)}, u32[]{:S(2)}, u32[]{:S(2)}) collective-permute-start(bf16[16,16,128]{2,1,0:T(8,128)(2,1)S(1)} %table.1), channel_id=1, source_target_pairs={{0,24},{4,28},{8,0},{12,4},{16,8},{20,12},{24,16},{28,20},{32,56},... | collective-permute-start | bytes 196616 | tf_op jit(solution)/shard_map/ppermute | solution.py:56
  78.5 8.2 %collective-permute-start.5 = (bf16[4,16,16,128]{3,2,1,0:T(8,128)(2,1)S(1)}, bf16[4,16,16,128]{3,2,1,0:T(8,128)(2,1)S(1)}, u32[]{:S(2)}, u32[]{:S(2)}) collective-permute-start(bf16[4,16,16,128]{3,2,1,0:T(8,128)(2,1)S(1)} %get-tuple-element.22), channel_id=1, source_target_pairs={{0,32},{4,36},{8,40},{12,44},{16,48},{20,52},{24,56},{28,60},{32,6... | collective-permute-start | bytes 786440 | tf_op jit(solution)/shard_map/ppermute | solution.py:56
  80.0 13.5 %collective-permute-start.4 = (bf16[4,16,16,128]{3,2,1,0:T(8,128)(2,1)S(1)}, bf16[4,16,16,128]{3,2,1,0:T(8,128)(2,1)S(1)}, u32[]{:S(2)}, u32[]{:S(2)}) collective-permute-start(bf16[4,16,16,128]{3,2,1,0:T(8,128)(2,1)S(1)} %get-tuple-element.22), channel_id=1, source_target_pairs={{0,64},{4,68},{8,72},{12,76},{16,80},{20,84},{24,88},{28,92},{32,9... | collective-permute-start | bytes 786440 | tf_op jit(solution)/shard_map/ppermute | solution.py:56
  82.4 11.1 %collective-permute-start.3 = (bf16[4,16,16,128]{3,2,1,0:T(8,128)(2,1)S(1)}, bf16[4,16,16,128]{3,2,1,0:T(8,128)(2,1)S(1)}, u32[]{:S(2)}, u32[]{:S(2)}) collective-permute-start(bf16[4,16,16,128]{3,2,1,0:T(8,128)(2,1)S(1)} %get-tuple-element.22), channel_id=1, source_target_pairs={{0,96},{4,100},{8,104},{12,108},{16,112},{20,116},{24,120},{28,124... | collective-permute-start | bytes 786440 | tf_op jit(solution)/shard_map/ppermute | solution.py:56
  93.6 23.5 %collective-permute-start.6 = (bf16[4,4,16,16,128]{4,3,2,1,0:T(8,128)(2,1)S(1)}, bf16[4,4,16,16,128]{4,3,2,1,0:T(8,128)(2,1)S(1)}, u32[]{:S(2)}, u32[]{:S(2)}) collective-permute-start(bf16[4,4,16,16,128]{4,3,2,1,0:T(8,128)(2,1)S(1)} %pad_maximum_fusion), channel_id=1, source_target_pairs={{0,3},{1,0},{2,1},{3,2},{4,7},{5,4},{6,5},{7,6},{8,11},{9,8},{10,9... | collective-permute-start | bytes 3145736 | tf_op jit(solution)/shard_map/ppermute | solution.py:60
  96.4 23.8 %collective-permute-start.7 = (bf16[4,4,16,16,128]{4,3,2,1,0:T(8,128)(2,1)S(1)}, bf16[4,4,16,16,128]{4,3,2,1,0:T(8,128)(2,1)S(1)}, u32[]{:S(2)}, u32[]{:S(2)}) collective-permute-start(bf16[4,4,16,16,128]{4,3,2,1,0:T(8,128)(2,1)S(1)} %pad_maximum_fusion), channel_id=1, source_target_pairs={{0,1},{1,2},{2,3},{3,0},{4,5},{5,6},{6,7},{7,4},{8,9},{9,10},{10,1... | collective-permute-start | bytes 3145736 | tf_op jit(solution)/shard_map/ppermute | solution.py:60
  96.4 49.7 %collective-permute-start.10 = (bf16[4,4,16,16,128]{4,3,2,1,0:T(8,128)(2,1)S(1)}, bf16[4,4,16,16,128]{4,3,2,1,0:T(8,128)(2,1)}, u32[]{:S(2)}, u32[]{:S(2)}) collective-permute-start(bf16[4,4,16,16,128]{4,3,2,1,0:T(8,128)(2,1)S(1)} %pad_maximum_fusion), channel_id=1, source_target_pairs={{0,4},{4,0},{8,12},{12,8},{16,20},{20,16},{24,28},{28,24},{32,36},... | collective-permute-start | bytes 3145736 | tf_op jit(solution)/shard_map/ppermute | solution.py:56
  117.1 29.1 %collective-permute-start.11 = (bf16[4,4,16,16,128]{4,3,2,1,0:T(8,128)(2,1)S(1)}, bf16[4,4,16,16,128]{4,3,2,1,0:T(8,128)(2,1)}, u32[]{:S(2)}, u32[]{:S(2)}) collective-permute-start(bf16[4,4,16,16,128]{4,3,2,1,0:T(8,128)(2,1)S(1)} %collective-permute-done.6), channel_id=1, source_target_pairs={{0,4},{4,0},{8,12},{12,8},{16,20},{20,16},{24,28},{28,24},{32,36},... | collective-permute-start | bytes 3145736 | tf_op jit(solution)/shard_map/ppermute | solution.py:56
  120.3 28.0 %collective-permute-start.12 = (bf16[4,4,16,16,128]{4,3,2,1,0:T(8,128)(2,1)S(1)}, bf16[4,4,16,16,128]{4,3,2,1,0:T(8,128)(2,1)}, u32[]{:S(2)}, u32[]{:S(2)}) collective-permute-start(bf16[4,4,16,16,128]{4,3,2,1,0:T(8,128)(2,1)S(1)} %collective-permute-done.7), channel_id=1, source_target_pairs={{0,4},{4,0},{8,12},{12,8},{16,20},{20,16},{24,28},{28,24},{32,36},... | collective-permute-start | bytes 3145736 | tf_op jit(solution)/shard_map/ppermute | solution.py:56
  123.3 13.7 %collective-permute-start.8 = (bf16[2,4,16,16,128]{4,3,2,1,0:T(8,128)(2,1)S(1)}, bf16[2,4,16,16,128]{4,3,2,1,0:T(8,128)(2,1)}, u32[]{:S(2)}, u32[]{:S(2)}) collective-permute-start(bf16[2,4,16,16,128]{4,3,2,1,0:T(8,128)(2,1)S(1)} %slice.8), channel_id=1, source_target_pairs={{0,3},{1,0},{2,1},{3,2},{4,7},{5,4},{6,5},{7,6},{8,11},{9,8},{10,9... | collective-permute-start | bytes 1572872 | tf_op jit(solution)/shard_map/ppermute | solution.py:60
  123.4 14.4 %collective-permute-start.9 = (bf16[2,4,16,16,128]{4,3,2,1,0:T(8,128)(2,1)S(1)}, bf16[2,4,16,16,128]{4,3,2,1,0:T(8,128)(2,1)}, u32[]{:S(2)}, u32[]{:S(2)}) collective-permute-start(bf16[2,4,16,16,128]{4,3,2,1,0:T(8,128)(2,1)S(1)} %slice.9), channel_id=1, source_target_pairs={{0,1},{1,2},{2,3},{3,0},{4,5},{5,6},{6,7},{7,4},{8,9},{9,10},{10,1... | collective-permute-start | bytes 1572872 | tf_op jit(solution)/shard_map/ppermute | solution.py:60
  136.9 11.4 %collective-permute-start.13 = (bf16[2,4,16,16,128]{4,3,2,1,0:T(8,128)(2,1)}, bf16[2,4,16,16,128]{4,3,2,1,0:T(8,128)(2,1)}, u32[]{:S(2)}, u32[]{:S(2)}) collective-permute-start(bf16[2,4,16,16,128]{4,3,2,1,0:T(8,128)(2,1)} %collective-permute-done.8), channel_id=1, source_target_pairs={{0,4},{4,0},{8,12},{12,8},{16,20},{20,16},{24,28},{28,24},{32,36},... | collective-permute-start | bytes 1572872 | tf_op jit(solution)/shard_map/ppermute | solution.py:56
  137.8 10.6 %collective-permute-start.14 = (bf16[2,4,16,16,128]{4,3,2,1,0:T(8,128)(2,1)}, bf16[2,4,16,16,128]{4,3,2,1,0:T(8,128)(2,1)}, u32[]{:S(2)}, u32[]{:S(2)}) collective-permute-start(bf16[2,4,16,16,128]{4,3,2,1,0:T(8,128)(2,1)} %collective-permute-done.9), channel_id=1, source_target_pairs={{0,4},{4,0},{8,12},{12,8},{16,20},{20,16},{24,28},{28,24},{32,36},... | collective-permute-start | bytes 1572872 | tf_op jit(solution)/shard_map/ppermute | solution.py:56
  139.2 1.0 copy-start.4
  141.2 0.8 copy-start.2
  142.0 1.0 copy-start.3
  146.2 9.1 %collective-permute-start.15 = (bf16[8,2,32,256]{3,2,1,0:T(8,128)(2,1)S(1)}, bf16[8,2,32,256]{3,2,1,0:T(8,128)(2,1)S(1)}, u32[]{:S(2)}, u32[]{:S(2)}) collective-permute-start(bf16[8,2,32,256]{3,2,1,0:T(8,128)(2,1)S(1)} %get-tuple-element.18), channel_id=1, source_target_pairs={{0,3},{1,0},{2,1},{3,2},{4,7},{5,4},{6,5},{7,6},{8,11},{9,8},{10,9... | collective-permute-start | bytes 786440 | tf_op jit(solution)/shard_map/ppermute | solution.py:60
  146.3 9.1 %collective-permute-start.16 = (bf16[8,2,32,256]{3,2,1,0:T(8,128)(2,1)S(1)}, bf16[8,2,32,256]{3,2,1,0:T(8,128)(2,1)S(1)}, u32[]{:S(2)}, u32[]{:S(2)}) collective-permute-start(bf16[8,2,32,256]{3,2,1,0:T(8,128)(2,1)S(1)} %get-tuple-element.19), channel_id=1, source_target_pairs={{0,2},{1,3},{2,0},{3,1},{4,6},{5,7},{6,4},{7,5},{8,10},{9,11},{10,... | collective-permute-start | bytes 786440 | tf_op jit(solution)/shard_map/ppermute | solution.py:60
  148.3 13.4 %collective-permute-start.17 = (bf16[8,2,32,256]{3,2,1,0:T(8,128)(2,1)S(1)}, bf16[8,2,32,256]{3,2,1,0:T(8,128)(2,1)S(1)}, u32[]{:S(2)}, u32[]{:S(2)}) collective-permute-start(bf16[8,2,32,256]{3,2,1,0:T(8,128)(2,1)S(1)} %get-tuple-element.20), channel_id=1, source_target_pairs={{0,1},{1,2},{2,3},{3,0},{4,5},{5,6},{6,7},{7,4},{8,9},{9,10},{10,1... | collective-permute-start | bytes 786440 | tf_op jit(solution)/shard_map/ppermute | solution.py:60

commit v2 on v1

--- a/solution.py
+++ b/solution.py
@@ -1,3 +1,5 @@
+import functools
+
 import jax
 import jax.numpy as jnp
 import numpy as np
@@ -6,6 +8,8 @@
 from jax.experimental.pallas import tpu as pltpu
 from jax.sharding import PartitionSpec as P
 
+
+SPLIT = (4, 4)
 
 F32 = jnp.float32
 BF16 = jnp.bfloat16
@@ -62,12 +66,12 @@
 
 def k_phase_kernel(ang_ref, out_ref):
     cos, sin = cos_sin(ang_ref[...])
-    cos = cos.astype(BF16)
-    sin = sin.astype(BF16)
-    out_ref[0:256, 0:512] = cos
-    out_ref[0:256, 512:1024] = -sin
-    out_ref[256:512, 0:512] = sin
-    out_ref[256:512, 512:1024] = cos
+    cos = jnp.swapaxes(cos.reshape(32, 8, 512), 0, 1).astype(BF16)
+    sin = jnp.swapaxes(sin.reshape(32, 8, 512), 0, 1).astype(BF16)
+    out_ref[:, 0, :, 0:512] = cos
+    out_ref[:, 0, :, 512:1024] = -sin
+    out_ref[:, 1, :, 0:512] = sin
+    out_ref[:, 1, :, 512:1024] = cos
 
 
 def k_phase_of(k_angle):
@@ -76,14 +80,14 @@
         k_phase_kernel,
         in_specs=[whole],
         out_specs=whole,
-        out_shape=jax.ShapeDtypeStruct((512, 1024), BF16),
+        out_shape=jax.ShapeDtypeStruct((8, 2, 32, 1024), BF16),
         cost_estimate=pl.CostEstimate(flops=1 << 23, bytes_accessed=2 << 20, transcendentals=0),
         compiler_params=limit(8),
         name="k_phase",
     )(k_angle)
 
 
-def k_kernel(phase_ref, g_ref, out_ref, g_in, middle, packed, in_sems, out_sems):
+def k_kernel(start, count, phase_ref, g_ref, out_ref, g_in, middle, packed, in_sems, out_sems):
     def load(rp):
         return pltpu.make_async_copy(g_ref.at[rp], g_in.at[rp], in_sems.at[rp])
 
@@ -95,46 +99,40 @@
             load(step * 4 + u).wait()
         for u in range(4):
             rp = step * 4 + u
-            part = jnp.dot(
-                phase_ref[...], g_in[rp].reshape(1024, 256), preferred_element_type=F32
-            )
+            phase = phase_ref[start : start + count].reshape(count * 64, 1024)
+            part = jnp.dot(phase, g_in[rp].reshape(1024, 256), preferred_element_type=F32)
             middle[rp] = part.astype(BF16)
         return carry
 
     lax.fori_loop(0, 4, some, 0)
 
-    def store(piece):
-        at = pl.ds(piece * 4, 4)
-        return pltpu.make_async_copy(packed.at[at], out_ref.at[at], out_sems.at[piece])
-
-    for piece in range(8):
-        for c in range(2):
-            at = c * 256 + 32 * piece
-            turned = jnp.swapaxes(middle[:, at : at + 32, :], 0, 1)
-            packed[piece * 4 : piece * 4 + 4, c * 8 : c * 8 + 8] = turned.reshape(4, 8, 16, 256)
-        store(piece).start()
-    for piece in range(8):
-        store(piece).wait()
-
-
-def k_transform(phase, g):
-    return pl.pallas_call(
-        k_kernel,
-        in_specs=[pl.BlockSpec(memory_space=VMEM), pl.BlockSpec(memory_space=pltpu.HBM)],
-        out_specs=pl.BlockSpec(memory_space=pltpu.HBM),
-        out_shape=jax.ShapeDtypeStruct((32, 16, 16, 256), BF16),
+    def store(at):
+        return pltpu.make_async_copy(packed.at[:, at], out_ref.at[:, at], out_sems.at[at])
+
+    for at in range(2 * count):
+        packed[:, at] = jnp.swapaxes(middle[:, at * 32 : at * 32 + 32, :], 0, 1)
+        store(at).start()
+    for at in range(2 * count):
+        store(at).wait()
+
+
+def k_transform(start, count, phase, g):
+    return pl.pallas_call(
+        functools.partial(k_kernel, start, count),
+        in_specs=[pl.BlockSpec(memory_space=VMEM), pl.BlockSpec(memory_space=pl.ANY)],
+        out_specs=pl.BlockSpec(memory_space=pl.ANY),
+        out_shape=jax.ShapeDtypeStruct((32, 2 * count, 16, 256), BF16),
         scratch_shapes=[
             VMEM((16, 2, 512, 256), BF16),
-            VMEM((16, 512, 256), BF16),
-            VMEM((32, 16, 16, 256), BF16),
+            VMEM((16, 64 * count, 256), BF16),
+            VMEM((32, 2 * count, 16, 256), BF16),
             pltpu.SemaphoreType.DMA((16,)),
-            pltpu.SemaphoreType.DMA((8,)),
+            pltpu.SemaphoreType.DMA((2 * count,)),
         ],
         cost_estimate=pl.CostEstimate(
-            flops=2 * 16 * 512 * 1024 * 256, bytes_accessed=12 << 20, transcendentals=0
+            flops=2 * 16 * 64 * count * 1024 * 256, bytes_accessed=10 << 20, transcendentals=0
         ),
-        compiler_params=limit(58),
-        name="k_transform",
+        compiler_params=limit(56),
     )(phase, g)
 
 
@@ -199,26 +197,20 @@
 
 
 def pick_kernel(me_ref, idx_ref, *refs):
-    parts, out_ref = refs[:10], refs[10]
-    table, spread, sems = refs[11:]
+    parts, outs = refs[:16], refs[16:18]
+    table, spread, blocks, sems, out_sems = refs[18:]
     k = pl.program_id(0)
+    slot = lax.rem(k, 2)
+
+    def store(out, at, place):
+        return pltpu.make_async_copy(blocks.at[place], out.at[at], out_sems.at[place])
 
     @pl.when(k == 0)
     def _():
-        copies = []
-        for cd in range(2):
-            own, y1, y3, y2a, y2b = parts[cd * 5 : cd * 5 + 5]
-            at = cd * 1024
-            for ref, start, size in (
-                (own, at, 256),
-                (y1, at + 256, 256),
-                (y2a, at + 512, 128),
-                (y2b, at + 640, 128),
-                (y3, at + 768, 256),
-            ):
-                copies.append(
-                    pltpu.make_async_copy(ref, table.at[pl.ds(start, size)], sems.at[len(copies)])
-                )
+        copies = [
+            pltpu.make_async_copy(part, table.at[pl.ds(at * 128, 128)], sems.at[at])
+            for at, part in enumerate(parts)
+        ]
         for copy in copies:
             copy.start()
         source = lax.broadcasted_iota(jnp.int32, (128, 1024), 0)
@@ -236,25 +228,45 @@
         tiles = jnp.stack([table[idx_ref[k, group * 8 + u]].astype(F32) for u in range(8)])
         groups.append(jnp.swapaxes(tiles, 0, 1).reshape(128, 128).astype(BF16))
     tiles = jnp.concatenate(groups, 0)
+
+    @pl.when(k >= 2)
+    def _():
+        store(outs[0], 0, slot).wait()
+
     for h in range(2):
         at = slice(h * 512, h * 512 + 512)
         wide = jnp.dot(tiles, spread[:, at], preferred_element_type=F32)
         for group in range(4):
             kept = jnp.where(same, wide[group * 128 : group * 128 + 128], 0.0)
-            out_ref[group, h * 128 : h * 128 + 128] = kept.astype(BF16)
+            blocks[slot, group, h * 128 : h * 128 + 128] = kept.astype(BF16)
+
+    @pl.when(k < SPLIT[0])
+    def _():
+        store(outs[0], k, slot).start()
+
+    @pl.when(k >= SPLIT[0])
+    def _():
+        store(outs[1], k - SPLIT[0], slot).start()
+
+    @pl.when(k == 7)
+    def _():
+        store(outs[1], 0, 0).wait()
+        store(outs[1], 0, 1).wait()
 
 
 def pick(me, idx, parts):
     return pl.pallas_call(
         pick_kernel,
         grid=(8,),
-        in_specs=[pl.BlockSpec(memory_space=SMEM)] * 2 + [pl.BlockSpec(memory_space=pl.ANY)] * 10,
-        out_specs=pl.BlockSpec((None, 4, 256, 512), lambda k: (k, 0, 0, 0)),
-        out_shape=jax.ShapeDtypeStruct((8, 4, 256, 512), BF16),
+        in_specs=[pl.BlockSpec(memory_space=SMEM)] * 2 + [pl.BlockSpec(memory_space=pl.ANY)] * 16,
+        out_specs=[pl.BlockSpec(memory_space=pl.ANY)] * 2,
+        out_shape=[jax.ShapeDtypeStruct((count, 4, 256, 512), BF16) for count in SPLIT],
         scratch_shapes=[
             VMEM((2048, 16, 128), BF16),
             VMEM((128, 1024), BF16),
-            pltpu.SemaphoreType.DMA((10,)),
+            VMEM((2, 4, 256, 512), BF16),
+            pltpu.SemaphoreType.DMA((16,)),
+            pltpu.SemaphoreType.DMA((2,)),
         ],
         cost_estimate=pl.CostEstimate(
             flops=2 * 32 * 128 * 128 * 1024, bytes_accessed=18 << 20, transcendentals=0
@@ -264,50 +276,55 @@
     )(me, idx, *parts)
 
 
-def q_kernel(phase_ref, data_ref, o0, o1, o2, o3, data, sems):
+def q_kernel(start, count, phase_ref, data_ref, o0, o1, o2, o3, data, phase, sems, phase_sem):
     outs = (o0, o1, o2, o3)
+    load_phase = pltpu.make_async_copy(phase_ref, phase, phase_sem)
+    load_phase.start()
 
     def load(k, part):
         return pltpu.make_async_copy(
-            data_ref.at[:, part * 8 + k], data.at[k, part], sems.at[k, part]
+            data_ref.at[:, 2 * (start + k) + part], data.at[k, part], sems.at[k, part]
         )
 
-    for k in range(8):
+    for k in range(count):
         for part in range(2):
             load(k, part).start()
-    for first in (0, 4):
-        for k in range(first, first + 4):
-            for part in range(2):
-                load(k, part).wait()
-        for k in range(first, first + 4):
-            stacked = data[k].reshape(1024, 256)
-            result = jnp.dot(phase_ref[...], stacked, preferred_element_type=F32).astype(BF16)
-            for part in range(2):
-                for bd in range(4):
-                    at = (part * 4 + bd) * 32
-                    outs[bd][k, part] = result[at : at + 32]
-
-
-def q_transform(phase, data):
+    load_phase.wait()
+    for k in range(count):
+        for part in range(2):
+            load(k, part).wait()
+    for k in range(count):
+        stacked = data[k].reshape(1024, 256)
+        result = jnp.dot(phase[...], stacked, preferred_element_type=F32).astype(BF16)
+        for part in range(2):
+            for bd in range(4):
+                at = (part * 4 + bd) * 32
+                outs[bd][k, part] = result[at : at + 32]
+
+
+def q_transform(start, count, phase, data):
     whole = pl.BlockSpec(memory_space=VMEM)
     return pl.pallas_call(
-        q_kernel,
-        in_specs=[whole, pl.BlockSpec(memory_space=pl.ANY)],
+        functools.partial(q_kernel, start, count),
+        in_specs=[pl.BlockSpec(memory_space=pl.ANY)] * 2,
         out_specs=[whole] * 4,
-        out_shape=[jax.ShapeDtypeStruct((8, 2, 32, 256), BF16)] * 4,
+        out_shape=[jax.ShapeDtypeStruct((count, 2, 32, 256), BF16)] * 4,
         scratch_shapes=[
-            VMEM((8, 2, 32, 16, 256), BF16),
-            pltpu.SemaphoreType.DMA((8, 2)),
+            VMEM((count, 2, 32, 16, 256), BF16),
+            VMEM((256, 1024), BF16),
+            pltpu.SemaphoreType.DMA((count, 2)),
+            pltpu.SemaphoreType.DMA,
         ],
         cost_estimate=pl.CostEstimate(
-            flops=2 * 8 * 256 * 1024 * 256, bytes_accessed=6 << 20, transcendentals=0
+            flops=2 * count * 256 * 1024 * 256, bytes_accessed=3 << 20, transcendentals=0
         ),
         compiler_params=limit(12),
-        name="q_transform",
     )(phase, data)
 
 
-def rotate_kernel(eig_ref, w_ref, a0, a1, a2, a3, out_ref, even, odd, merged, done):
+def rotate_kernel(start, count, eig_ref, w_ref, a0, a1, a2, a3, *refs):
+    before = refs[0] if start else None
+    out_ref, even, odd, merged, done = refs[1 if start else 0 :]
     arrays = (a0, a1, a2, a3)
     quarter = lax.broadcasted_iota(jnp.int32, (8, 128), 1) // 32
 
@@ -323,7 +340,7 @@
             blocks = []
             for part in range(2):
                 for at in range(4):
-                    block = eig_ref[k, part * 32 : part * 32 + 32]
+                    block = eig_ref[k + start, part * 32 : part * 32 + 32]
                     blocks.append(block if at == low else jnp.zeros_like(block))
             half = jnp.dot(both, jnp.concatenate(blocks, 0), preferred_element_type=F32)
             for hi in range(2):
@@ -352,43 +369,39 @@
                 )
         done[k] = merged[...].astype(BF16)
 
+    slots = (even, odd)
     first(0, even)
-
-    def two(step, carry):
-        first(2 * step + 1, odd)
-        second(2 * step, even)
-        first(2 * step + 2, even)
-        second(2 * step + 1, odd)
-        return carry
-
-    lax.fori_loop(0, 3, two, 0)
-    first(7, odd)
-    second(6, even)
-    second(7, odd)
-    out_ref[...] = jnp.swapaxes(done[...], 0, 1)
-
-
-def rotate(eig, picked, arrays):
+    for k in range(count):
+        if k + 1 < count:
+            first(k + 1, slots[(k + 1) % 2])
+        second(k, slots[k % 2])
+    if start:
+        out_ref[...] = jnp.swapaxes(jnp.concatenate([before[...], done[...]], 0), 0, 1)
+    else:
+        out_ref[...] = done[...]
+
+
+def rotate(start, count, eig, picked, arrays, before=None):
     whole = pl.BlockSpec(memory_space=VMEM)
-    return pl.pallas_call(
-        rotate_kernel,
-        in_specs=[whole] * 6,
+    out = (32, 8, 1024) if start else (count, 32, 1024)
+    return pl.pallas_call(
+        functools.partial(rotate_kernel, start, count),
+        in_specs=[whole] * (7 if start else 6),
         out_specs=whole,
-        out_shape=jax.ShapeDtypeStruct((32, 8, 1024), BF16),
+        out_shape=jax.ShapeDtypeStruct(out, BF16),
         scratch_shapes=[
             VMEM((4, 512, 128), F32),
             VMEM((4, 512, 128), F32),
             VMEM((32, 1024), F32),
-            VMEM((8, 32, 1024), BF16),
+            VMEM((count, 32, 1024), BF16),
         ],
         cost_estimate=pl.CostEstimate(
-            flops=2 * 8 * 4 * (256 * 256 * 256 + 256 * 512 * 128),
-            bytes_accessed=12 << 20,
+            flops=2 * count * 4 * (256 * 256 * 256 + 256 * 512 * 128),
+            bytes_accessed=6 << 20,
             transcendentals=0,
         ),
-        compiler_params=limit(12),
-        name="rotate",
-    )(eig, picked, *arrays)
+        compiler_params=limit(10),
+    )(eig, picked, *arrays, *([before] if start else []))
 
 
 def shards(g_wannier, k_angle, q_angle, eig_k, eig_kq, mask_k, mask_kq, owner, kq_local):
@@ -406,14 +419,17 @@
     from_z = []
     for d in (1, 2, 3):
         from_z.append(row_shift(along_x, dz=-d))
-    along_z = jnp.stack([along_x] + from_z)
-    y1 = blk_shift(along_z, -1)
-    y3 = blk_shift(along_z, 1)
-    y2a = blk_shift(y1[0:2], -1)
-    y2b = blk_shift(y3[2:4], 1)
-    own = [along_z, y1, y3, y2a, y2b]
-    other = [row_shift(part, dc=1) for part in own]
-    parts = [part.reshape(-1, 16, 128) for part in own + other]
+    halves = (jnp.stack([along_x, from_z[0]]), jnp.stack(from_z[1:]))
+    own = {(0, 0): halves[0], (0, 1): halves[1]}
+    for y, half, dy in ((1, 0, -1), (3, 1, 1), (1, 1, -1), (3, 0, 1)):
+        own[y, half] = blk_shift(halves[half], dy)
+    own[2, 0] = blk_shift(own[1, 0], -1)
+    own[2, 1] = blk_shift(own[3, 1], 1)
+    order = [(y, half) for y in range(4) for half in range(2)]
+    parts = [own[at] for at in order]
+    for y, half in order:
+        parts.append(row_shift(own[y, half], dc=1))
+    parts = [part.reshape(-1, 16, 128) for part in parts]
 
     own_row = owner.reshape(8, 32) // 4
     c_off = (own_row - c) % 2
@@ -423,16 +439,20 @@
     idx = (((c_off * 4 + y_off) * 4 + z_off) * 4 + x_off) * 16 + kq_local.reshape(8, 32)
 
     k_phase = k_phase_of(k_angle)
-    sent = k_transform(k_phase, g_wannier)
+    sent = k_transform(0, 8, k_phase, g_wannier)
     taken = lax.all_to_all(sent, "row", split_axis=0, concat_axis=0, tiled=True)
 
     phase, eig = prep(me, q_angle, eig_k, mask_k)
     picked = pick(me, idx, parts)
-    outs = q_transform(phase, taken)
-    arrays = {0: outs[0]}
-    for d in (1, 2, 3):
-        arrays[(-d) % 4] = blk_shift(outs[d], d)
-    return rotate(eig, picked, [arrays[off] for off in range(4)])
+    result = None
+    for par in range(2):
+        outs = q_transform(par * SPLIT[0], SPLIT[par], phase, taken)
+        arrays = {0: outs[0]}
+        for d in (1, 2, 3):
+            arrays[(-d) % 4] = blk_shift(outs[d], d)
+        order = [arrays[off] for off in range(4)]
+        result = rotate(par * SPLIT[0], SPLIT[par], eig, picked[par], order, result)
+    return result
 
 
 def solution(mesh):

time: 168 us -> 164 us (0.976)
  waiting for transfers between devices: 97 us -> 84.5 us
  starting transfers between devices: 35.4 us -> 42.6 us
  Pallas kernels: 27.6 us -> 30 us
    ppermute x7 -> x12, waiting for transfers between devices: 37.4 us -> 25 us  [blk_shift(): return lax.ppermute(value, 'blk', [(y, (y + dy) % 4) for y in range(4)])]
    ppermute x7 -> x12, starting transfers between devices: 6.48 us -> 15.3 us  [blk_shift(): return lax.ppermute(value, 'blk', [(y, (y + dy) % 4) for y in range(4)])]
    ppermute x11 -> x14, starting transfers between devices: 19.3 us -> 17.7 us  [row_shift(): return lax.ppermute(value, 'row', pairs)]
    pallas_call x3 -> x5, Pallas kernels: 18.6 us -> 19.7 us  [the longest x1 10.2 us: k_transform(): pl.pallas_call(functools.partial(k_kernel, start, count), in_specs=[pl.Bl...]
    unnamed x22 -> x26, local copies, waits for them, and re-layouts: 6.52 us -> 6.28 us
    ppermute x11 -> x14, waiting for transfers between devices: 59.6 us -> 59.4 us  [row_shift(): return lax.ppermute(value, 'row', pairs)]
  transfers between devices with their start and end apart: 19 -> 27, of which waited for: 8 -> 8; matrix products, arithmetic and copies ran while one was open for 0% -> 0% of each run, Pallas kernels for 7% -> 10%
where the time goes in v2:
time: 164 us
  waiting for transfers between devices  84.5 us (52%)
  starting transfers between devices  42.6 us (26%)
  Pallas kernels  30 us (18%)
  local copies, waits for them, and re-layouts  6.28 us (4%)
    ppermute x14, waiting for transfers between devices, row_shift(): return lax.ppermute(value, 'row', pairs)  59.4 us
    ppermute x12, waiting for transfers between devices, blk_shift(): return lax.ppermute(value, 'blk', [(y, (y + dy) % 4) for y in range(4)])  25 us
    ppermute x14, starting transfers between devices, row_shift(): return lax.ppermute(value, 'row', pairs)  17.7 us
    ppermute x12, starting transfers between devices, blk_shift(): return lax.ppermute(value, 'blk', [(y, (y + dy) % 4) for y in range(4)])  15.3 us
    pallas_call x1, Pallas kernels, k_transform(): pl.pallas_call(functools.partial(k_kernel, start, count), in_specs=[pl.Bl...  10.2 us
    all_to_all x1, starting transfers between devices, shards(): taken = lax.all_to_all(sent, 'row', split_axis=0, concat_axis=0, tiled=True)  9.61 us
    pallas_call x1, Pallas kernels, pick(): pl.pallas_call(pick_kernel, grid=(8,), in_specs=[pl.BlockSpec(memory_spac...  8.12 us
    unnamed x26, local copies, waits for them, and re-layouts  6.28 us
  transfers between devices with their start and end apart: 27, of which 8 were waited for; matrix products, arithmetic and copies ran while one was open for 0% of the time, Pallas kernels for 10%

profile of v2, /device:TPU:1, one launch (start us, length us, event | category | flops | bytes accessed | tf_op | source)
XLA Modules:
  0.0 163.9 jit_solution(987004490819190097)
XLA Ops:
  0.0 0.9 copy-done.7
  1.0 0.7 copy-done.9
  1.6 0.3 table.1
  1.9 1.0 copy-done.1
  3.0 0.8 k_phase.1.phase_ref
  3.9 1.0 copy-done
  4.8 10.2 %shard_map.91 = bf16[32,16,16,256]{3,2,1,0:T(8,128)(2,1)} custom-call(bf16[8,2,32,1024]{3,2,1,0:T(8,128)(2,1)} %copy-done, bf16[16,2,512,256]{3,2,1,0:T(8,128)(2,1)} %g_ref.1), custom_call_target="tpu_custom_call" | custom-call | flops 4294967296 | bytes 10485760 | tf_op jit(solution)/shard_map/pallas_call | solution.py:120
  15.0 9.6 %all-to-all-start = ((bf16[32,16,16,256]{3,2,1,0:T(8,128)(2,1)}), bf16[32,16,16,256]{3,2,1,0:T(8,128)(2,1)}, u32[]{:S(2)}, u32[]{:S(2)}) async-start(bf16[32,16,16,256]{3,2,1,0:T(8,128)(2,1)} %shard_map.91), calls=%async_computation | async-start | bytes 8388608 | tf_op jit(solution)/shard_map/all_to_all | solution.py:443
  24.7 1.4 collective-permute-start.2
  26.1 2.4 %collective-permute-start.1 = (bf16[16,16,128]{2,1,0:T(8,128)(2,1)S(1)}, bf16[16,16,128]{2,1,0:T(8,128)(2,1)S(1)}, u32[]{:S(2)}, u32[]{:S(2)}) collective-permute-start(bf16[16,16,128]{2,1,0:T(8,128)(2,1)S(1)} %table.1), channel_id=1, source_target_pairs={{0,16},{4,20},{8,24},{12,28},{16,0},{20,4},{24,8},{28,12},{32,48},... | collective-permute-start | bytes 196616 | tf_op jit(solution)/shard_map/ppermute | solution.py:60
  28.5 1.2 collective-permute-start
  29.7 44.7 %collective-permute-done.2 = bf16[16,16,128]{2,1,0:T(8,128)(2,1)S(1)} collective-permute-done((bf16[16,16,128]{2,1,0:T(8,128)(2,1)S(1)}, bf16[16,16,128]{2,1,0:T(8,128)(2,1)S(1)}, u32[]{:S(2)}, u32[]{:S(2)}) %collective-permute-start.2) | collective-permute-done | bytes 65568 | tf_op jit(solution)/shard_map/ppermute | solution.py:60
  74.4 4.3 %collective-permute-done.1 = bf16[16,16,128]{2,1,0:T(8,128)(2,1)S(1)} collective-permute-done((bf16[16,16,128]{2,1,0:T(8,128)(2,1)S(1)}, bf16[16,16,128]{2,1,0:T(8,128)(2,1)S(1)}, u32[]{:S(2)}, u32[]{:S(2)}) %collective-permute-start.1) | collective-permute-done | bytes 65568 | tf_op jit(solution)/shard_map/ppermute | solution.py:60
  78.7 2.3 %collective-permute-start.4 = (bf16[4,16,16,128]{3,2,1,0:T(8,128)(2,1)S(1)}, bf16[4,16,16,128]{3,2,1,0:T(8,128)(2,1)S(1)}, u32[]{:S(2)}, u32[]{:S(2)}) collective-permute-start(bf16[4,16,16,128]{3,2,1,0:T(8,128)(2,1)S(1)} %get-tuple-element.34), channel_id=1, source_target_pairs={{0,64},{4,68},{8,72},{12,76},{16,80},{20,84},{24,88},{28,92},{32,9... | collective-permute-start | bytes 786440 | tf_op jit(solution)/shard_map/ppermute | solution.py:60
  81.1 1.0 collective-permute-start.5
  82.1 1.7 %collective-permute-start.3 = (bf16[4,16,16,128]{3,2,1,0:T(8,128)(2,1)S(1)}, bf16[4,16,16,128]{3,2,1,0:T(8,128)(2,1)S(1)}, u32[]{:S(2)}, u32[]{:S(2)}) collective-permute-start(bf16[4,16,16,128]{3,2,1,0:T(8,128)(2,1)S(1)} %get-tuple-element.34), channel_id=1, source_target_pairs={{0,96},{4,100},{8,104},{12,108},{16,112},{20,116},{24,120},{28,124... | collective-permute-start | bytes 786440 | tf_op jit(solution)/shard_map/ppermute | solution.py:60
  83.8 3.5 %collective-permute-done.4 = bf16[4,16,16,128]{3,2,1,0:T(8,128)(2,1)S(1)} collective-permute-done((bf16[4,16,16,128]{3,2,1,0:T(8,128)(2,1)S(1)}, bf16[4,16,16,128]{3,2,1,0:T(8,128)(2,1)S(1)}, u32[]{:S(2)}, u32[]{:S(2)}) %collective-permute-start.4) | collective-permute-done | bytes 262176 | tf_op jit(solution)/shard_map/ppermute | solution.py:60
  87.3 6.9 %collective-permute-done.5 = bf16[4,16,16,128]{3,2,1,0:T(8,128)(2,1)S(1)} collective-permute-done((bf16[4,16,16,128]{3,2,1,0:T(8,128)(2,1)S(1)}, bf16[4,16,16,128]{3,2,1,0:T(8,128)(2,1)S(1)}, u32[]{:S(2)}, u32[]{:S(2)}) %collective-permute-start.5) | collective-permute-done | bytes 262176 | tf_op jit(solution)/shard_map/ppermute | solution.py:60
  94.2 0.6 collective-permute-start.13
  94.8 1.3 collective-permute-start.9
  96.1 1.4 collective-permute-start.7
  97.6 1.5 collective-permute-start.6
  99.1 0.9 collective-permute-start.12
  100.0 9.5 %collective-permute-done.9 = bf16[2,4,16,16,128]{4,3,2,1,0:T(8,128)(2,1)S(1)} collective-permute-done((bf16[2,4,16,16,128]{4,3,2,1,0:T(8,128)(2,1)S(1)}, bf16[2,4,16,16,128]{4,3,2,1,0:T(8,128)(2,1)S(1)}, u32[]{:S(2)}, u32[]{:S(2)}) %collective-permute-start.9) | collective-permute-done | bytes 524320 | tf_op jit(solution)/shard_map/ppermute | solution.py:64
  109.5 1.4 collective-permute-start.19
  110.9 0.1 collective-permute-start.10
  111.0 9.6 %collective-permute-done.6 = bf16[2,4,16,16,128]{4,3,2,1,0:T(8,128)(2,1)} collective-permute-done((bf16[2,4,16,16,128]{4,3,2,1,0:T(8,128)(2,1)S(1)}, bf16[2,4,16,16,128]{4,3,2,1,0:T(8,128)(2,1)}, u32[]{:S(2)}, u32[]{:S(2)}) %collective-permute-start.6) | collective-permute-done | bytes 524320 | tf_op jit(solution)/shard_map/ppermute | solution.py:64
  120.5 2.7 %collective-permute-start.8 = (bf16[2,4,16,16,128]{4,3,2,1,0:T(8,128)(2,1)}, bf16[2,4,16,16,128]{4,3,2,1,0:T(8,128)(2,1)}, u32[]{:S(2)}, u32[]{:S(2)}) collective-permute-start(bf16[2,4,16,16,128]{4,3,2,1,0:T(8,128)(2,1)} %collective-permute-done.6), channel_id=1, source_target_pairs={{0,3},{1,0},{2,1},{3,2},{4,7},{5,4},{6,5},{7,6},{8,11},{9,8},{10,9... | collective-permute-start | bytes 1572872 | tf_op jit(solution)/shard_map/ppermute | solution.py:64
  123.3 0.8 copy-done.2
  124.1 1.4 collective-permute-start.15
  125.5 0.8 copy-done.4
  126.3 0.5 collective-permute-start.14
  126.8 5.3 %collective-permute-done.10 = bf16[2,4,16,16,128]{4,3,2,1,0:T(8,128)(2,1)} collective-permute-done((bf16[2,4,16,16,128]{4,3,2,1,0:T(8,128)(2,1)S(1)}, bf16[2,4,16,16,128]{4,3,2,1,0:T(8,128)(2,1)}, u32[]{:S(2)}, u32[]{:S(2)}) %collective-permute-start.10) | collective-permute-done | bytes 524320 | tf_op jit(solution)/shard_map/ppermute | solution.py:64
  132.1 0.9 collective-permute-start.17
  133.0 0.7 collective-permute-done.8
  133.7 2.0 %collective-permute-start.16 = (bf16[2,4,16,16,128]{4,3,2,1,0:T(8,128)(2,1)}, bf16[2,4,16,16,128]{4,3,2,1,0:T(8,128)(2,1)}, u32[]{:S(2)}, u32[]{:S(2)}) collective-permute-start(bf16[2,4,16,16,128]{4,3,2,1,0:T(8,128)(2,1)} %collective-permute-done.8), channel_id=1, source_target_pairs={{0,4},{4,0},{8,12},{12,8},{16,20},{20,16},{24,28},{28,24},{32,36},... | collective-permute-start | bytes 1572872 | tf_op jit(solution)/shard_map/ppermute | solution.py:60
  135.8 0.9 copy-done.6
  136.7 1.0 prep.1
  137.8 2.4 %shard_map.93 = (bf16[4,2,32,256]{3,2,1,0:T(8,128)(2,1)S(1)}, bf16[4,2,32,256]{3,2,1,0:T(8,128)(2,1)S(1)}, bf16[4,2,32,256]{3,2,1,0:T(8,128)(2,1)S(1)}, bf16[4,2,32,256]{3,2,1,0:T(8,128)(2,1)S(1)}) custom-call(bf16[256,1024]{1,0:T(8,128)(2,1)S(1)} %get-tuple-element.22.phase_ref, bf16[32,16,16,256]{3,2,1,0:T(8,128)(2,1)} %all-to-all-done.data_ref), custom_call_target="tpu_custom_call" | custom-call | flops 536870912 | bytes 3145728 | tf_op jit(solution)/shard_map/pallas_call | solution.py:307
  140.3 3.5 %collective-permute-start.23 = (bf16[4,2,32,256]{3,2,1,0:T(8,128)(2,1)S(1)}, bf16[4,2,32,256]{3,2,1,0:T(8,128)(2,1)S(1)}, u32[]{:S(2)}, u32[]{:S(2)}) collective-permute-start(bf16[4,2,32,256]{3,2,1,0:T(8,128)(2,1)S(1)} %get-tuple-element.30), channel_id=1, source_target_pairs={{0,3},{1,0},{2,1},{3,2},{4,7},{5,4},{6,5},{7,6},{8,11},{9,8},{10,9... | collective-permute-start | bytes 393224 | tf_op jit(solution)/shard_map/ppermute | solution.py:64
  143.8 0.3 collective-permute-start.24
  144.1 0.6 collective-permute-start.25
  144.7 2.3 %shard_map.92 = (bf16[4,2,32,256]{3,2,1,0:T(8,128)(2,1)S(1)}, bf16[4,2,32,256]{3,2,1,0:T(8,128)(2,1)S(1)}, bf16[4,2,32,256]{3,2,1,0:T(8,128)(2,1)S(1)}, bf16[4,2,32,256]{3,2,1,0:T(8,128)(2,1)S(1)}) custom-call(bf16[256,1024]{1,0:T(8,128)(2,1)S(1)} %get-tuple-element.22.phase_ref, bf16[32,16,16,256]{3,2,1,0:T(8,128)(2,1)} %all-to-all-done.data_ref), custom_call_target="tpu_custom_call" | custom-call | flops 536870912 | bytes 3145728 | tf_op jit(solution)/shard_map/pallas_call | solution.py:307
  147.0 2.2 %collective-permute-start.20 = (bf16[4,2,32,256]{3,2,1,0:T(8,128)(2,1)S(1)}, bf16[4,2,32,256]{3,2,1,0:T(8,128)(2,1)S(1)}, u32[]{:S(2)}, u32[]{:S(2)}) collective-permute-start(bf16[4,2,32,256]{3,2,1,0:T(8,128)(2,1)S(1)} %get-tuple-element.25), channel_id=1, source_target_pairs={{0,3},{1,0},{2,1},{3,2},{4,7},{5,4},{6,5},{7,6},{8,11},{9,8},{10,9... | collective-permute-start | bytes 393224 | tf_op jit(solution)/shard_map/ppermute | solution.py:64
  149.3 1.7 %collective-permute-start.21 = (bf16[4,2,32,256]{3,2,1,0:T(8,128)(2,1)S(1)}, bf16[4,2,32,256]{3,2,1,0:T(8,128)(2,1)S(1)}, u32[]{:S(2)}, u32[]{:S(2)}) collective-permute-start(bf16[4,2,32,256]{3,2,1,0:T(8,128)(2,1)S(1)} %get-tuple-element.26), channel_id=1, source_target_pairs={{0,2},{1,3},{2,0},{3,1},{4,6},{5,7},{6,4},{7,5},{8,10},{9,11},{10,... | collective-permute-start | bytes 393224 | tf_op jit(solution)/shard_map/ppermute | solution.py:64
  150.9 8.1 %pick.1 = (bf16[4,4,256,512]{3,2,1,0:T(8,128)(2,1)S(1)}, bf16[4,4,256,512]{3,2,1,0:T(8,128)(2,1)S(1)}) custom-call(s32[4]{0:T(128)S(1)} %pad_add_fusion.me_ref, s32[8,32]{1,0:T(8,128)S(1)} %fusion.9.idx_ref, bf16[128,16,128]{2,1,0:T(8,128)(2,1)S(1)} %bitcast.32, bf16[128,16,128]{2,1,0:T(8,128)(2,1)S(1)} %bitcast.31, bf16[128,16,128]{2,1,0:T(8,128)(2,1)} %bitcast.16.refs_2_, ...), custom_call_target="tpu_custom_call" | custom-call | flops 1073741824 | bytes 18874368 | tf_op jit(solution)/shard_map/pick/pallas_call | solution.py:258
  159.1 1.9 %shard_map.94.refs_0_ = bf16[4,32,1024]{2,1,0:T(8,128)(2,1)S(1)} custom-call(bf16[8,64,256]{2,1,0:T(8,128)(2,1)S(1)} %get-tuple-element.19.eig_ref, bf16[4,4,256,512]{3,2,1,0:T(8,128)(2,1)S(1)} %get-tuple-element.28.w_ref, bf16[4,2,32,256]{3,2,1,0:T(8,128)(2,1)S(1)} %get-tuple-element.29.a0, bf16[4,2,32,256]{3,2,1,0:T(8,128)(2,1)S(1)} %collective-permute-done.23.a1, ...), custom_call_target="tpu_custom_call" | custom-call | flops 1073741824 | bytes 6291456 | tf_op jit(solution)/shard_map/pallas_call | solution.py:387
  161.1 2.8 %shard_map.95 = bf16[32,8,1024]{2,1,0:T(8,128)(2,1)} custom-call(bf16[8,64,256]{2,1,0:T(8,128)(2,1)S(1)} %get-tuple-element.19.eig_ref, bf16[4,4,256,512]{3,2,1,0:T(8,128)(2,1)S(1)} %get-tuple-element.21.w_ref, bf16[4,2,32,256]{3,2,1,0:T(8,128)(2,1)S(1)} %get-tuple-element.24.a0, bf16[4,2,32,256]{3,2,1,0:T(8,128)(2,1)S(1)} %collective-permute-done.20.a1, ...), custom_call_target="tpu_custom_call" | custom-call | flops 1073741824 | bytes 6291456 | tf_op jit(solution)/shard_map/pallas_call | solution.py:387
  (46 shorter events, 0.4 us)
Async XLA Ops:
  0.0 0.9 copy-start.7
  1.0 0.7 copy-start.9
  1.9 1.0 copy-start.1
  3.8 1.0 copy-start
  15.0 120.8 %copy-start.8 = (bf16[8,2,32,32]{3,2,1,0:T(8,128)(2,1)S(1)}, bf16[8,2,32,32]{3,2,1,0:T(8,128)(2,1)}, u32[]{:S(2)}) copy-start(bf16[8,2,32,32]{3,2,1,0:T(8,128)(2,1)} %eig_ref.2) | copy-start | bytes 98308
  15.0 120.8 %copy-start.10 = (s32[8,32]{1,0:T(8,128)S(1)}, s32[8,32]{1,0:T(8,128)}, u32[]{:S(2)}) copy-start(s32[8,32]{1,0:T(8,128)} %mask_ref.2) | copy-start | bytes 3076
  15.0 122.8 %all-to-all-start = ((bf16[32,16,16,256]{3,2,1,0:T(8,128)(2,1)}), bf16[32,16,16,256]{3,2,1,0:T(8,128)(2,1)}, u32[]{:S(2)}, u32[]{:S(2)}) async-start(bf16[32,16,16,256]{3,2,1,0:T(8,128)(2,1)} %shard_map.91), calls=%async_computation | async-start | bytes 8388608 | tf_op jit(solution)/shard_map/all_to_all | solution.py:443
  24.7 119.1 %copy-start.11 = (s32[1,8,32,1]{2,3,1,0:T(1,128)S(1)}, s32[1,8,32,1]{2,3,1,0:T(1,128)}, u32[]{:S(2)}) copy-start(s32[1,8,32,1]{2,3,1,0:T(1,128)} %param.17) | copy-start | bytes 3076
  24.7 119.1 %copy-start.12 = (s32[1,8,32,1]{2,3,1,0:T(1,128)S(1)}, s32[1,8,32,1]{2,3,1,0:T(1,128)}, u32[]{:S(2)}) copy-start(s32[1,8,32,1]{2,3,1,0:T(1,128)} %param.16) | copy-start | bytes 3076
  24.7 49.7 %collective-permute-start.2 = (bf16[16,16,128]{2,1,0:T(8,128)(2,1)S(1)}, bf16[16,16,128]{2,1,0:T(8,128)(2,1)S(1)}, u32[]{:S(2)}, u32[]{:S(2)}) collective-permute-start(bf16[16,16,128]{2,1,0:T(8,128)(2,1)S(1)} %table.1), channel_id=1, source_target_pairs={{0,8},{4,12},{8,16},{12,20},{16,24},{20,28},{24,0},{28,4},{32,40},... | collective-permute-start | bytes 196616 | tf_op jit(solution)/shard_map/ppermute | solution.py:60
  26.1 52.6 %collective-permute-start.1 = (bf16[16,16,128]{2,1,0:T(8,128)(2,1)S(1)}, bf16[16,16,128]{2,1,0:T(8,128)(2,1)S(1)}, u32[]{:S(2)}, u32[]{:S(2)}) collective-permute-start(bf16[16,16,128]{2,1,0:T(8,128)(2,1)S(1)} %table.1), channel_id=1, source_target_pairs={{0,16},{4,20},{8,24},{12,28},{16,0},{20,4},{24,8},{28,12},{32,48},... | collective-permute-start | bytes 196616 | tf_op jit(solution)/shard_map/ppermute | solution.py:60
  28.5 50.2 %collective-permute-start = (bf16[16,16,128]{2,1,0:T(8,128)(2,1)S(1)}, bf16[16,16,128]{2,1,0:T(8,128)(2,1)S(1)}, u32[]{:S(2)}, u32[]{:S(2)}) collective-permute-start(bf16[16,16,128]{2,1,0:T(8,128)(2,1)S(1)} %table.1), channel_id=1, source_target_pairs={{0,24},{4,28},{8,0},{12,4},{16,8},{20,12},{24,16},{28,20},{32,56},... | collective-permute-start | bytes 196616 | tf_op jit(solution)/shard_map/ppermute | solution.py:60
  78.7 8.5 %collective-permute-start.4 = (bf16[4,16,16,128]{3,2,1,0:T(8,128)(2,1)S(1)}, bf16[4,16,16,128]{3,2,1,0:T(8,128)(2,1)S(1)}, u32[]{:S(2)}, u32[]{:S(2)}) collective-permute-start(bf16[4,16,16,128]{3,2,1,0:T(8,128)(2,1)S(1)} %get-tuple-element.34), channel_id=1, source_target_pairs={{0,64},{4,68},{8,72},{12,76},{16,80},{20,84},{24,88},{28,92},{32,9... | collective-permute-start | bytes 786440 | tf_op jit(solution)/shard_map/ppermute | solution.py:60
  81.1 13.1 %collective-permute-start.5 = (bf16[4,16,16,128]{3,2,1,0:T(8,128)(2,1)S(1)}, bf16[4,16,16,128]{3,2,1,0:T(8,128)(2,1)S(1)}, u32[]{:S(2)}, u32[]{:S(2)}) collective-permute-start(bf16[4,16,16,128]{3,2,1,0:T(8,128)(2,1)S(1)} %get-tuple-element.34), channel_id=1, source_target_pairs={{0,32},{4,36},{8,40},{12,44},{16,48},{20,52},{24,56},{28,60},{32,6... | collective-permute-start | bytes 786440 | tf_op jit(solution)/shard_map/ppermute | solution.py:60
  82.1 15.5 %collective-permute-start.3 = (bf16[4,16,16,128]{3,2,1,0:T(8,128)(2,1)S(1)}, bf16[4,16,16,128]{3,2,1,0:T(8,128)(2,1)S(1)}, u32[]{:S(2)}, u32[]{:S(2)}) collective-permute-start(bf16[4,16,16,128]{3,2,1,0:T(8,128)(2,1)S(1)} %get-tuple-element.34), channel_id=1, source_target_pairs={{0,96},{4,100},{8,104},{12,108},{16,112},{20,116},{24,120},{28,124... | collective-permute-start | bytes 786440 | tf_op jit(solution)/shard_map/ppermute | solution.py:60
  94.2 5.8 %collective-permute-start.13 = (bf16[2,4,16,16,128]{4,3,2,1,0:T(8,128)(2,1)S(1)}, bf16[2,4,16,16,128]{4,3,2,1,0:T(8,128)(2,1)S(1)}, u32[]{:S(2)}, u32[]{:S(2)}) collective-permute-start(bf16[2,4,16,16,128]{4,3,2,1,0:T(8,128)(2,1)S(1)} %pad_maximum_fusion.1), channel_id=1, source_target_pairs={{0,4},{4,0},{8,12},{12,8},{16,20},{20,16},{24,28},{28,24},{32,36},... | collective-permute-start | bytes 1572872 | tf_op jit(solution)/shard_map/ppermute | solution.py:60
  94.8 14.7 %collective-permute-start.9 = (bf16[2,4,16,16,128]{4,3,2,1,0:T(8,128)(2,1)S(1)}, bf16[2,4,16,16,128]{4,3,2,1,0:T(8,128)(2,1)S(1)}, u32[]{:S(2)}, u32[]{:S(2)}) collective-permute-start(bf16[2,4,16,16,128]{4,3,2,1,0:T(8,128)(2,1)S(1)} %pad_maximum_fusion.1), channel_id=1, source_target_pairs={{0,1},{1,2},{2,3},{3,0},{4,5},{5,6},{6,7},{7,4},{8,9},{9,10},{10,1... | collective-permute-start | bytes 1572872 | tf_op jit(solution)/shard_map/ppermute | solution.py:64
  96.1 14.8 %collective-permute-start.7 = (bf16[2,4,16,16,128]{4,3,2,1,0:T(8,128)(2,1)S(1)}, bf16[2,4,16,16,128]{4,3,2,1,0:T(8,128)(2,1)S(1)}, u32[]{:S(2)}, u32[]{:S(2)}) collective-permute-start(bf16[2,4,16,16,128]{4,3,2,1,0:T(8,128)(2,1)S(1)} %pad_maximum_fusion.1), channel_id=1, source_target_pairs={{0,3},{1,0},{2,1},{3,2},{4,7},{5,4},{6,5},{7,6},{8,11},{9,8},{10,9... | collective-permute-start | bytes 1572872 | tf_op jit(solution)/shard_map/ppermute | solution.py:64
  97.6 23.0 %collective-permute-start.6 = (bf16[2,4,16,16,128]{4,3,2,1,0:T(8,128)(2,1)S(1)}, bf16[2,4,16,16,128]{4,3,2,1,0:T(8,128)(2,1)}, u32[]{:S(2)}, u32[]{:S(2)}) collective-permute-start(bf16[2,4,16,16,128]{4,3,2,1,0:T(8,128)(2,1)S(1)} %pad_maximum_fusion), channel_id=1, source_target_pairs={{0,3},{1,0},{2,1},{3,2},{4,7},{5,4},{6,5},{7,6},{8,11},{9,8},{10,9... | collective-permute-start | bytes 1572872 | tf_op jit(solution)/shard_map/ppermute | solution.py:64
  99.1 24.1 %collective-permute-start.12 = (bf16[2,4,16,16,128]{4,3,2,1,0:T(8,128)(2,1)S(1)}, bf16[2,4,16,16,128]{4,3,2,1,0:T(8,128)(2,1)S(1)}, u32[]{:S(2)}, u32[]{:S(2)}) collective-permute-start(bf16[2,4,16,16,128]{4,3,2,1,0:T(8,128)(2,1)S(1)} %pad_maximum_fusion), channel_id=1, source_target_pairs={{0,4},{4,0},{8,12},{12,8},{16,20},{20,16},{24,28},{28,24},{32,36},... | collective-permute-start | bytes 1572872 | tf_op jit(solution)/shard_map/ppermute | solution.py:60
  100.0 25.5 %collective-permute-start.11 = (bf16[2,4,16,16,128]{4,3,2,1,0:T(8,128)(2,1)S(1)}, bf16[2,4,16,16,128]{4,3,2,1,0:T(8,128)(2,1)}, u32[]{:S(2)}, u32[]{:S(2)}) collective-permute-start(bf16[2,4,16,16,128]{4,3,2,1,0:T(8,128)(2,1)S(1)} %pad_maximum_fusion), channel_id=1, source_target_pairs={{0,1},{1,2},{2,3},{3,0},{4,5},{5,6},{6,7},{7,4},{8,9},{9,10},{10,1... | collective-permute-start | bytes 1572872 | tf_op jit(solution)/shard_map/ppermute | solution.py:64
  109.5 16.0 %collective-permute-start.19 = (bf16[2,4,16,16,128]{4,3,2,1,0:T(8,128)(2,1)S(1)}, bf16[2,4,16,16,128]{4,3,2,1,0:T(8,128)(2,1)S(1)}, u32[]{:S(2)}, u32[]{:S(2)}) collective-permute-start(bf16[2,4,16,16,128]{4,3,2,1,0:T(8,128)(2,1)S(1)} %collective-permute-done.9), channel_id=1, source_target_pairs={{0,4},{4,0},{8,12},{12,8},{16,20},{20,16},{24,28},{28,24},{32,36},... | collective-permute-start | bytes 1572872 | tf_op jit(solution)/shard_map/ppermute | solution.py:60
  110.9 21.2 %collective-permute-start.10 = (bf16[2,4,16,16,128]{4,3,2,1,0:T(8,128)(2,1)S(1)}, bf16[2,4,16,16,128]{4,3,2,1,0:T(8,128)(2,1)}, u32[]{:S(2)}, u32[]{:S(2)}) collective-permute-start(bf16[2,4,16,16,128]{4,3,2,1,0:T(8,128)(2,1)S(1)} %collective-permute-done.9), channel_id=1, source_target_pairs={{0,1},{1,2},{2,3},{3,0},{4,5},{5,6},{6,7},{7,4},{8,9},{9,10},{10,1... | collective-permute-start | bytes 1572872 | tf_op jit(solution)/shard_map/ppermute | solution.py:64
  120.5 13.1 %collective-permute-start.8 = (bf16[2,4,16,16,128]{4,3,2,1,0:T(8,128)(2,1)}, bf16[2,4,16,16,128]{4,3,2,1,0:T(8,128)(2,1)}, u32[]{:S(2)}, u32[]{:S(2)}) collective-permute-start(bf16[2,4,16,16,128]{4,3,2,1,0:T(8,128)(2,1)} %collective-permute-done.6), channel_id=1, source_target_pairs={{0,3},{1,0},{2,1},{3,2},{4,7},{5,4},{6,5},{7,6},{8,11},{9,8},{10,9... | collective-permute-start | bytes 1572872 | tf_op jit(solution)/shard_map/ppermute | solution.py:64
  123.3 0.8 copy-start.2
  124.1 16.2 %collective-permute-start.15 = (bf16[2,4,16,16,128]{4,3,2,1,0:T(8,128)(2,1)S(1)}, bf16[2,4,16,16,128]{4,3,2,1,0:T(8,128)(2,1)}, u32[]{:S(2)}, u32[]{:S(2)}) collective-permute-start(bf16[2,4,16,16,128]{4,3,2,1,0:T(8,128)(2,1)S(1)} %collective-permute-done.7), channel_id=1, source_target_pairs={{0,4},{4,0},{8,12},{12,8},{16,20},{20,16},{24,28},{28,24},{32,36},... | collective-permute-start | bytes 1572872 | tf_op jit(solution)/shard_map/ppermute | solution.py:60
  125.5 18.3 %collective-permute-start.18 = (bf16[2,4,16,16,128]{4,3,2,1,0:T(8,128)(2,1)}, bf16[2,4,16,16,128]{4,3,2,1,0:T(8,128)(2,1)}, u32[]{:S(2)}, u32[]{:S(2)}) collective-permute-start(bf16[2,4,16,16,128]{4,3,2,1,0:T(8,128)(2,1)} %collective-permute-done.11), channel_id=1, source_target_pairs={{0,4},{4,0},{8,12},{12,8},{16,20},{20,16},{24,28},{28,24},{32,36},... | collective-permute-start | bytes 1572872 | tf_op jit(solution)/shard_map/ppermute | solution.py:60
  125.5 0.8 copy-start.4
  126.3 17.7 %collective-permute-start.14 = (bf16[2,4,16,16,128]{4,3,2,1,0:T(8,128)(2,1)}, bf16[2,4,16,16,128]{4,3,2,1,0:T(8,128)(2,1)}, u32[]{:S(2)}, u32[]{:S(2)}) collective-permute-start(bf16[2,4,16,16,128]{4,3,2,1,0:T(8,128)(2,1)} %collective-permute-done.6), channel_id=1, source_target_pairs={{0,4},{4,0},{8,12},{12,8},{16,20},{20,16},{24,28},{28,24},{32,36},... | collective-permute-start | bytes 1572872 | tf_op jit(solution)/shard_map/ppermute | solution.py:60
  132.1 14.9 %collective-permute-start.17 = (bf16[2,4,16,16,128]{4,3,2,1,0:T(8,128)(2,1)}, bf16[2,4,16,16,128]{4,3,2,1,0:T(8,128)(2,1)}, u32[]{:S(2)}, u32[]{:S(2)}) collective-permute-start(bf16[2,4,16,16,128]{4,3,2,1,0:T(8,128)(2,1)} %collective-permute-done.10), channel_id=1, source_target_pairs={{0,4},{4,0},{8,12},{12,8},{16,20},{20,16},{24,28},{28,24},{32,36},... | collective-permute-start | bytes 1572872 | tf_op jit(solution)/shard_map/ppermute | solution.py:60
  133.7 15.6 %collective-permute-start.16 = (bf16[2,4,16,16,128]{4,3,2,1,0:T(8,128)(2,1)}, bf16[2,4,16,16,128]{4,3,2,1,0:T(8,128)(2,1)}, u32[]{:S(2)}, u32[]{:S(2)}) collective-permute-start(bf16[2,4,16,16,128]{4,3,2,1,0:T(8,128)(2,1)} %collective-permute-done.8), channel_id=1, source_target_pairs={{0,4},{4,0},{8,12},{12,8},{16,20},{20,16},{24,28},{28,24},{32,36},... | collective-permute-start | bytes 1572872 | tf_op jit(solution)/shard_map/ppermute | solution.py:60
  135.8 1.0 copy-start.6
  137.8 13.1 %copy-start.3 = (bf16[2,4,16,16,128]{4,3,2,1,0:T(8,128)(2,1)S(1)}, bf16[2,4,16,16,128]{4,3,2,1,0:T(8,128)(2,1)}, u32[]{:S(2)}) copy-start(bf16[2,4,16,16,128]{4,3,2,1,0:T(8,128)(2,1)} %copy-done.2) | copy-start | bytes 1572868
  137.8 13.1 %copy-start.5 = (bf16[2,4,16,16,128]{4,3,2,1,0:T(8,128)(2,1)S(1)}, bf16[2,4,16,16,128]{4,3,2,1,0:T(8,128)(2,1)}, u32[]{:S(2)}) copy-start(bf16[2,4,16,16,128]{4,3,2,1,0:T(8,128)(2,1)} %copy-done.4) | copy-start | bytes 1572868
  140.3 10.7 %collective-permute-start.23 = (bf16[4,2,32,256]{3,2,1,0:T(8,128)(2,1)S(1)}, bf16[4,2,32,256]{3,2,1,0:T(8,128)(2,1)S(1)}, u32[]{:S(2)}, u32[]{:S(2)}) collective-permute-start(bf16[4,2,32,256]{3,2,1,0:T(8,128)(2,1)S(1)} %get-tuple-element.30), channel_id=1, source_target_pairs={{0,3},{1,0},{2,1},{3,2},{4,7},{5,4},{6,5},{7,6},{8,11},{9,8},{10,9... | collective-permute-start | bytes 393224 | tf_op jit(solution)/shard_map/ppermute | solution.py:64
  143.8 15.3 %collective-permute-start.24 = (bf16[4,2,32,256]{3,2,1,0:T(8,128)(2,1)S(1)}, bf16[4,2,32,256]{3,2,1,0:T(8,128)(2,1)S(1)}, u32[]{:S(2)}, u32[]{:S(2)}) collective-permute-start(bf16[4,2,32,256]{3,2,1,0:T(8,128)(2,1)S(1)} %get-tuple-element.31), channel_id=1, source_target_pairs={{0,2},{1,3},{2,0},{3,1},{4,6},{5,7},{6,4},{7,5},{8,10},{9,11},{10,... | collective-permute-start | bytes 393224 | tf_op jit(solution)/shard_map/ppermute | solution.py:64
  144.1 15.0 %collective-permute-start.25 = (bf16[4,2,32,256]{3,2,1,0:T(8,128)(2,1)S(1)}, bf16[4,2,32,256]{3,2,1,0:T(8,128)(2,1)S(1)}, u32[]{:S(2)}, u32[]{:S(2)}) collective-permute-start(bf16[4,2,32,256]{3,2,1,0:T(8,128)(2,1)S(1)} %get-tuple-element.32), channel_id=1, source_target_pairs={{0,1},{1,2},{2,3},{3,0},{4,5},{5,6},{6,7},{7,4},{8,9},{9,10},{10,1... | collective-permute-start | bytes 393224 | tf_op jit(solution)/shard_map/ppermute | solution.py:64
  147.0 14.0 %collective-permute-start.20 = (bf16[4,2,32,256]{3,2,1,0:T(8,128)(2,1)S(1)}, bf16[4,2,32,256]{3,2,1,0:T(8,128)(2,1)S(1)}, u32[]{:S(2)}, u32[]{:S(2)}) collective-permute-start(bf16[4,2,32,256]{3,2,1,0:T(8,128)(2,1)S(1)} %get-tuple-element.25), channel_id=1, source_target_pairs={{0,3},{1,0},{2,1},{3,2},{4,7},{5,4},{6,5},{7,6},{8,11},{9,8},{10,9... | collective-permute-start | bytes 393224 | tf_op jit(solution)/shard_map/ppermute | solution.py:64
  149.3 11.8 %collective-permute-start.21 = (bf16[4,2,32,256]{3,2,1,0:T(8,128)(2,1)S(1)}, bf16[4,2,32,256]{3,2,1,0:T(8,128)(2,1)S(1)}, u32[]{:S(2)}, u32[]{:S(2)}) collective-permute-start(bf16[4,2,32,256]{3,2,1,0:T(8,128)(2,1)S(1)} %get-tuple-element.26), channel_id=1, source_target_pairs={{0,2},{1,3},{2,0},{3,1},{4,6},{5,7},{6,4},{7,5},{8,10},{9,11},{10,... | collective-permute-start | bytes 393224 | tf_op jit(solution)/shard_map/ppermute | solution.py:64
  150.9 10.1 %collective-permute-start.22 = (bf16[4,2,32,256]{3,2,1,0:T(8,128)(2,1)S(1)}, bf16[4,2,32,256]{3,2,1,0:T(8,128)(2,1)S(1)}, u32[]{:S(2)}, u32[]{:S(2)}) collective-permute-start(bf16[4,2,32,256]{3,2,1,0:T(8,128)(2,1)S(1)} %get-tuple-element.27), channel_id=1, source_target_pairs={{0,1},{1,2},{2,3},{3,0},{4,5},{5,6},{6,7},{7,4},{8,9},{9,10},{10,1... | collective-permute-start | bytes 393224 | tf_op jit(solution)/shard_map/ppermute | solution.py:64

commit v3 on v2

--- a/solution.py
+++ b/solution.py
@@ -291,9 +291,10 @@
             load(k, part).start()
     load_phase.wait()
     for k in range(count):
-        for part in range(2):
-            load(k, part).wait()
-    for k in range(count):
+        if k % 2 == 0:
+            for later in range(k, min(k + 2, count)):
+                for part in range(2):
+                    load(later, part).wait()
         stacked = data[k].reshape(1024, 256)
         result = jnp.dot(phase[...], stacked, preferred_element_type=F32).astype(BF16)
         for part in range(2):
@@ -322,9 +323,8 @@
     )(phase, data)
 
 
-def rotate_kernel(start, count, eig_ref, w_ref, a0, a1, a2, a3, *refs):
-    before = refs[0] if start else None
-    out_ref, even, odd, merged, done = refs[1 if start else 0 :]
+def rotate_kernel(eig_ref, w0, w1, a0, a1, a2, a3, out_ref, even, odd, merged, done):
+    start, count = 0, 8
     arrays = (a0, a1, a2, a3)
     quarter = lax.broadcasted_iota(jnp.int32, (8, 128), 1) // 32
 
@@ -354,7 +354,7 @@
     def second(k, halves):
         for group in range(4):
             rotated = jnp.dot(
-                w_ref[k, group], halves[group].astype(BF16), preferred_element_type=F32
+                (w0, w1)[k // 4][k % 4, group], halves[group].astype(BF16), preferred_element_type=F32
             )
             square = rotated * rotated
             square = square + pltpu.roll(square, 32, 1)
@@ -375,33 +375,30 @@
         if k + 1 < count:
             first(k + 1, slots[(k + 1) % 2])
         second(k, slots[k % 2])
-    if start:
-        out_ref[...] = jnp.swapaxes(jnp.concatenate([before[...], done[...]], 0), 0, 1)
-    else:
-        out_ref[...] = done[...]
-
-
-def rotate(start, count, eig, picked, arrays, before=None):
+    out_ref[...] = jnp.swapaxes(done[...], 0, 1)
+
+
+def rotate(eig, picked, arrays):
     whole = pl.BlockSpec(memory_space=VMEM)
-    out = (32, 8, 1024) if start else (count, 32, 1024)
-    return pl.pallas_call(
-        functools.partial(rotate_kernel, start, count),
-        in_specs=[whole] * (7 if start else 6),
+    return pl.pallas_call(
+        rotate_kernel,
+        in_specs=[whole] * 7,
         out_specs=whole,
-        out_shape=jax.ShapeDtypeStruct(out, BF16),
+        out_shape=jax.ShapeDtypeStruct((32, 8, 1024), BF16),
         scratch_shapes=[
             VMEM((4, 512, 128), F32),
             VMEM((4, 512, 128), F32),
             VMEM((32, 1024), F32),
-            VMEM((count, 32, 1024), BF16),
+            VMEM((8, 32, 1024), BF16),
         ],
         cost_estimate=pl.CostEstimate(
-            flops=2 * count * 4 * (256 * 256 * 256 + 256 * 512 * 128),
-            bytes_accessed=6 << 20,
+            flops=2 * 8 * 4 * (256 * 256 * 256 + 256 * 512 * 128),
+            bytes_accessed=12 << 20,
             transcendentals=0,
         ),
         compiler_params=limit(10),
-    )(eig, picked, *arrays, *([before] if start else []))
+        name="rotate",
+    )(eig, *picked, *arrays)
 
 
 def shards(g_wannier, k_angle, q_angle, eig_k, eig_kq, mask_k, mask_kq, owner, kq_local):
@@ -444,15 +441,11 @@
 
     phase, eig = prep(me, q_angle, eig_k, mask_k)
     picked = pick(me, idx, parts)
-    result = None
-    for par in range(2):
-        outs = q_transform(par * SPLIT[0], SPLIT[par], phase, taken)
-        arrays = {0: outs[0]}
-        for d in (1, 2, 3):
-            arrays[(-d) % 4] = blk_shift(outs[d], d)
-        order = [arrays[off] for off in range(4)]
-        result = rotate(par * SPLIT[0], SPLIT[par], eig, picked[par], order, result)
-    return result
+    outs = q_transform(0, 8, phase, taken)
+    arrays = {0: outs[0]}
+    for d in (1, 2, 3):
+        arrays[(-d) % 4] = blk_shift(outs[d], d)
+    return rotate(eig, picked, [arrays[off] for off in range(4)])
 
 
 def solution(mesh):

time: 164 us -> 165 us (level)
  waiting for transfers between devices: 84.5 us -> 90.5 us
  starting transfers between devices: 42.6 us -> 38.6 us
    ppermute x12 -> x9, waiting for transfers between devices: 25 us -> 31.1 us  [blk_shift(): return lax.ppermute(value, 'blk', [(y, (y + dy) % 4) for y in range(4)])]
    ppermute x12 -> x9, starting transfers between devices: 15.3 us -> 11.2 us  [blk_shift(): return lax.ppermute(value, 'blk', [(y, (y + dy) % 4) for y in range(4)])]
    pallas_call x2 -> x1, Pallas kernels: 4.76 us -> 3.23 us  [q_transform(): pl.pallas_call(functools.partial(q_kernel, start, count), in_specs=[pl.Bl...]
    pallas_call x2 -> x1, Pallas kernels: 4.75 us -> 4.63 us  [rotate(): pl.pallas_call(rotate_kernel, in_specs=[whole] * 7, out_specs=whole, out_...]
  transfers between devices with their start and end apart: 27 -> 24, of which waited for: 8 -> 10; matrix products, arithmetic and copies ran while one was open for 0% -> 0% of each run, Pallas kernels for 10% -> 8%
where the time goes in v3:
time: 165 us; the launch traced here: 164 us
  waiting for transfers between devices  90.5 us (55%)
  starting transfers between devices  38.6 us (23%)
  Pallas kernels  28.4 us (17%)
  local copies, waits for them, and re-layouts  6.27 us (4%)
    ppermute x14, waiting for transfers between devices, row_shift(): return lax.ppermute(value, 'row', pairs)  59.4 us
    ppermute x9, waiting for transfers between devices, blk_shift(): return lax.ppermute(value, 'blk', [(y, (y + dy) % 4) for y in range(4)])  31.1 us
    ppermute x14, starting transfers between devices, row_shift(): return lax.ppermute(value, 'row', pairs)  17.7 us
    ppermute x9, starting transfers between devices, blk_shift(): return lax.ppermute(value, 'blk', [(y, (y + dy) % 4) for y in range(4)])  11.2 us
    pallas_call x1, Pallas kernels, k_transform(): pl.pallas_call(functools.partial(k_kernel, start, count), in_specs=[pl.Bl...  10.2 us
    all_to_all x1, starting transfers between devices, shards(): taken = lax.all_to_all(sent, 'row', split_axis=0, concat_axis=0, tiled=True)  9.63 us
    pallas_call x1, Pallas kernels, pick(): pl.pallas_call(pick_kernel, grid=(8,), in_specs=[pl.BlockSpec(memory_spac...  8.12 us
    unnamed x26, local copies, waits for them, and re-layouts  6.27 us
  transfers between devices with their start and end apart: 24, of which 10 were waited for; matrix products, arithmetic and copies ran while one was open for 0% of the time, Pallas kernels for 8%

profile of v3, /device:TPU:1, one launch (start us, length us, event | category | flops | bytes accessed | tf_op | source)
XLA Modules:
  0.0 164.2 jit_solution(613629543437947166)
XLA Ops:
  0.0 0.9 copy-done.7
  1.0 0.7 copy-done.9
  1.6 0.3 table.1
  1.9 1.0 copy-done.1
  3.0 0.8 k_phase.1.phase_ref
  3.9 1.0 copy-done
  4.9 10.2 %shard_map.91 = bf16[32,16,16,256]{3,2,1,0:T(8,128)(2,1)} custom-call(bf16[8,2,32,1024]{3,2,1,0:T(8,128)(2,1)} %copy-done, bf16[16,2,512,256]{3,2,1,0:T(8,128)(2,1)} %g_ref.1), custom_call_target="tpu_custom_call" | custom-call | flops 4294967296 | bytes 10485760 | tf_op jit(solution)/shard_map/pallas_call | solution.py:120
  15.1 9.6 %all-to-all-start = ((bf16[32,16,16,256]{3,2,1,0:T(8,128)(2,1)}), bf16[32,16,16,256]{3,2,1,0:T(8,128)(2,1)}, u32[]{:S(2)}, u32[]{:S(2)}) async-start(bf16[32,16,16,256]{3,2,1,0:T(8,128)(2,1)} %shard_map.91), calls=%async_computation | async-start | bytes 8388608 | tf_op jit(solution)/shard_map/all_to_all | solution.py:440
  24.7 1.4 collective-permute-start.2
  26.2 2.4 %collective-permute-start.1 = (bf16[16,16,128]{2,1,0:T(8,128)(2,1)S(1)}, bf16[16,16,128]{2,1,0:T(8,128)(2,1)S(1)}, u32[]{:S(2)}, u32[]{:S(2)}) collective-permute-start(bf16[16,16,128]{2,1,0:T(8,128)(2,1)S(1)} %table.1), channel_id=1, source_target_pairs={{0,16},{4,20},{8,24},{12,28},{16,0},{20,4},{24,8},{28,12},{32,48},... | collective-permute-start | bytes 196616 | tf_op jit(solution)/shard_map/ppermute | solution.py:60
  28.6 1.2 collective-permute-start
  29.7 44.7 %collective-permute-done.2 = bf16[16,16,128]{2,1,0:T(8,128)(2,1)S(1)} collective-permute-done((bf16[16,16,128]{2,1,0:T(8,128)(2,1)S(1)}, bf16[16,16,128]{2,1,0:T(8,128)(2,1)S(1)}, u32[]{:S(2)}, u32[]{:S(2)}) %collective-permute-start.2) | collective-permute-done | bytes 65568 | tf_op jit(solution)/shard_map/ppermute | solution.py:60
  74.4 4.3 %collective-permute-done.1 = bf16[16,16,128]{2,1,0:T(8,128)(2,1)S(1)} collective-permute-done((bf16[16,16,128]{2,1,0:T(8,128)(2,1)S(1)}, bf16[16,16,128]{2,1,0:T(8,128)(2,1)S(1)}, u32[]{:S(2)}, u32[]{:S(2)}) %collective-permute-start.1) | collective-permute-done | bytes 65568 | tf_op jit(solution)/shard_map/ppermute | solution.py:60
  78.8 2.3 %collective-permute-start.4 = (bf16[4,16,16,128]{3,2,1,0:T(8,128)(2,1)S(1)}, bf16[4,16,16,128]{3,2,1,0:T(8,128)(2,1)S(1)}, u32[]{:S(2)}, u32[]{:S(2)}) collective-permute-start(bf16[4,16,16,128]{3,2,1,0:T(8,128)(2,1)S(1)} %get-tuple-element.26), channel_id=1, source_target_pairs={{0,64},{4,68},{8,72},{12,76},{16,80},{20,84},{24,88},{28,92},{32,9... | collective-permute-start | bytes 786440 | tf_op jit(solution)/shard_map/ppermute | solution.py:60
  81.1 1.0 collective-permute-start.5
  82.1 1.7 %collective-permute-start.3 = (bf16[4,16,16,128]{3,2,1,0:T(8,128)(2,1)S(1)}, bf16[4,16,16,128]{3,2,1,0:T(8,128)(2,1)S(1)}, u32[]{:S(2)}, u32[]{:S(2)}) collective-permute-start(bf16[4,16,16,128]{3,2,1,0:T(8,128)(2,1)S(1)} %get-tuple-element.26), channel_id=1, source_target_pairs={{0,96},{4,100},{8,104},{12,108},{16,112},{20,116},{24,120},{28,124... | collective-permute-start | bytes 786440 | tf_op jit(solution)/shard_map/ppermute | solution.py:60
  83.8 3.5 %collective-permute-done.4 = bf16[4,16,16,128]{3,2,1,0:T(8,128)(2,1)S(1)} collective-permute-done((bf16[4,16,16,128]{3,2,1,0:T(8,128)(2,1)S(1)}, bf16[4,16,16,128]{3,2,1,0:T(8,128)(2,1)S(1)}, u32[]{:S(2)}, u32[]{:S(2)}) %collective-permute-start.4) | collective-permute-done | bytes 262176 | tf_op jit(solution)/shard_map/ppermute | solution.py:60
  87.3 6.9 %collective-permute-done.5 = bf16[4,16,16,128]{3,2,1,0:T(8,128)(2,1)S(1)} collective-permute-done((bf16[4,16,16,128]{3,2,1,0:T(8,128)(2,1)S(1)}, bf16[4,16,16,128]{3,2,1,0:T(8,128)(2,1)S(1)}, u32[]{:S(2)}, u32[]{:S(2)}) %collective-permute-start.5) | collective-permute-done | bytes 262176 | tf_op jit(solution)/shard_map/ppermute | solution.py:60
  94.2 0.1 pad_maximum_fusion.1
  94.3 0.6 collective-permute-start.13
  94.8 1.3 collective-permute-start.9
  96.1 1.4 collective-permute-start.7
  97.6 0.1 pad_maximum_fusion
  97.6 1.5 collective-permute-start.6
  99.2 0.9 collective-permute-start.12
  100.1 9.5 %collective-permute-done.9 = bf16[2,4,16,16,128]{4,3,2,1,0:T(8,128)(2,1)S(1)} collective-permute-done((bf16[2,4,16,16,128]{4,3,2,1,0:T(8,128)(2,1)S(1)}, bf16[2,4,16,16,128]{4,3,2,1,0:T(8,128)(2,1)S(1)}, u32[]{:S(2)}, u32[]{:S(2)}) %collective-permute-start.9) | collective-permute-done | bytes 524320 | tf_op jit(solution)/shard_map/ppermute | solution.py:64
  109.6 1.4 collective-permute-start.19
  110.9 0.1 collective-permute-start.10
  111.0 9.6 %collective-permute-done.6 = bf16[2,4,16,16,128]{4,3,2,1,0:T(8,128)(2,1)} collective-permute-done((bf16[2,4,16,16,128]{4,3,2,1,0:T(8,128)(2,1)S(1)}, bf16[2,4,16,16,128]{4,3,2,1,0:T(8,128)(2,1)}, u32[]{:S(2)}, u32[]{:S(2)}) %collective-permute-start.6) | collective-permute-done | bytes 524320 | tf_op jit(solution)/shard_map/ppermute | solution.py:64
  120.6 2.7 %collective-permute-start.8 = (bf16[2,4,16,16,128]{4,3,2,1,0:T(8,128)(2,1)}, bf16[2,4,16,16,128]{4,3,2,1,0:T(8,128)(2,1)}, u32[]{:S(2)}, u32[]{:S(2)}) collective-permute-start(bf16[2,4,16,16,128]{4,3,2,1,0:T(8,128)(2,1)} %collective-permute-done.6), channel_id=1, source_target_pairs={{0,3},{1,0},{2,1},{3,2},{4,7},{5,4},{6,5},{7,6},{8,11},{9,8},{10,9... | collective-permute-start | bytes 1572872 | tf_op jit(solution)/shard_map/ppermute | solution.py:64
  123.3 0.8 copy-done.2
  124.1 1.4 collective-permute-start.15
  125.6 0.8 copy-done.4
  126.4 0.5 collective-permute-start.14
  126.9 5.3 %collective-permute-done.10 = bf16[2,4,16,16,128]{4,3,2,1,0:T(8,128)(2,1)} collective-permute-done((bf16[2,4,16,16,128]{4,3,2,1,0:T(8,128)(2,1)S(1)}, bf16[2,4,16,16,128]{4,3,2,1,0:T(8,128)(2,1)}, u32[]{:S(2)}, u32[]{:S(2)}) %collective-permute-start.10) | collective-permute-done | bytes 524320 | tf_op jit(solution)/shard_map/ppermute | solution.py:64
  132.1 0.9 collective-permute-start.17
  133.0 0.7 collective-permute-done.8
  133.7 2.0 %collective-permute-start.16 = (bf16[2,4,16,16,128]{4,3,2,1,0:T(8,128)(2,1)}, bf16[2,4,16,16,128]{4,3,2,1,0:T(8,128)(2,1)}, u32[]{:S(2)}, u32[]{:S(2)}) collective-permute-start(bf16[2,4,16,16,128]{4,3,2,1,0:T(8,128)(2,1)} %collective-permute-done.8), channel_id=1, source_target_pairs={{0,4},{4,0},{8,12},{12,8},{16,20},{20,16},{24,28},{28,24},{32,36},... | collective-permute-start | bytes 1572872 | tf_op jit(solution)/shard_map/ppermute | solution.py:60
  135.8 0.1 pad_add_fusion.me_ref
  135.8 0.9 copy-done.6
  136.8 1.0 prep.1
  137.9 3.2 %shard_map.92 = (bf16[8,2,32,256]{3,2,1,0:T(8,128)(2,1)S(1)}, bf16[8,2,32,256]{3,2,1,0:T(8,128)(2,1)S(1)}, bf16[8,2,32,256]{3,2,1,0:T(8,128)(2,1)S(1)}, bf16[8,2,32,256]{3,2,1,0:T(8,128)(2,1)S(1)}) custom-call(bf16[256,1024]{1,0:T(8,128)(2,1)S(1)} %get-tuple-element.19.phase_ref, bf16[32,16,16,256]{3,2,1,0:T(8,128)(2,1)} %all-to-all-done.data_ref), custom_call_target="tpu_custom_call" | custom-call | flops 1073741824 | bytes 3145728 | tf_op jit(solution)/shard_map/pallas_call | solution.py:308
  141.1 3.5 %collective-permute-start.20 = (bf16[8,2,32,256]{3,2,1,0:T(8,128)(2,1)S(1)}, bf16[8,2,32,256]{3,2,1,0:T(8,128)(2,1)S(1)}, u32[]{:S(2)}, u32[]{:S(2)}) collective-permute-start(bf16[8,2,32,256]{3,2,1,0:T(8,128)(2,1)S(1)} %get-tuple-element.22), channel_id=1, source_target_pairs={{0,3},{1,0},{2,1},{3,2},{4,7},{5,4},{6,5},{7,6},{8,11},{9,8},{10,9... | collective-permute-start | bytes 786440 | tf_op jit(solution)/shard_map/ppermute | solution.py:64
  144.6 0.7 collective-permute-start.22
  145.4 8.1 %pick.1 = (bf16[4,4,256,512]{3,2,1,0:T(8,128)(2,1)S(1)}, bf16[4,4,256,512]{3,2,1,0:T(8,128)(2,1)S(1)}) custom-call(s32[4]{0:T(128)S(1)} %pad_add_fusion.me_ref, s32[8,32]{1,0:T(8,128)S(1)} %fusion.9.idx_ref, bf16[128,16,128]{2,1,0:T(8,128)(2,1)S(1)} %bitcast.32, bf16[128,16,128]{2,1,0:T(8,128)(2,1)S(1)} %bitcast.31, bf16[128,16,128]{2,1,0:T(8,128)(2,1)} %bitcast.16.refs_2_, ...), custom_call_target="tpu_custom_call" | custom-call | flops 1073741824 | bytes 18874368 | tf_op jit(solution)/shard_map/pick/pallas_call | solution.py:258
  153.5 2.4 %collective-permute-done.20.a1 = bf16[8,2,32,256]{3,2,1,0:T(8,128)(2,1)S(1)} collective-permute-done((bf16[8,2,32,256]{3,2,1,0:T(8,128)(2,1)S(1)}, bf16[8,2,32,256]{3,2,1,0:T(8,128)(2,1)S(1)}, u32[]{:S(2)}, u32[]{:S(2)}) %collective-permute-start.20) | collective-permute-done | bytes 262176 | tf_op jit(solution)/shard_map/ppermute | solution.py:64
  155.9 3.6 %collective-permute-done.22.a3 = bf16[8,2,32,256]{3,2,1,0:T(8,128)(2,1)S(1)} collective-permute-done((bf16[8,2,32,256]{3,2,1,0:T(8,128)(2,1)S(1)}, bf16[8,2,32,256]{3,2,1,0:T(8,128)(2,1)S(1)}, u32[]{:S(2)}, u32[]{:S(2)}) %collective-permute-start.22) | collective-permute-done | bytes 262176 | tf_op jit(solution)/shard_map/ppermute | solution.py:64
  159.5 4.6 %rotate.1 = bf16[32,8,1024]{2,1,0:T(8,128)(2,1)} custom-call(bf16[8,64,256]{2,1,0:T(8,128)(2,1)S(1)} %get-tuple-element.15.eig_ref, bf16[4,4,256,512]{3,2,1,0:T(8,128)(2,1)S(1)} %get-tuple-element.17.w0, bf16[4,4,256,512]{3,2,1,0:T(8,128)(2,1)S(1)} %get-tuple-element.18.w1, bf16[8,2,32,256]{3,2,1,0:T(8,128)(2,1)S(1)} %get-tuple-element.21.a0, ...), custom_call_target="tpu_custom_call" | custom-call | flops 2147483648 | bytes 12582912 | tf_op jit(solution)/shard_map/rotate/pallas_call | solution.py:383
  (38 shorter events, 0.2 us)
Async XLA Ops:
  0.0 0.9 copy-start.7
  1.0 0.7 copy-start.9
  1.9 1.0 copy-start.1
  3.8 1.0 copy-start
  15.1 120.8 %copy-start.8 = (bf16[8,2,32,32]{3,2,1,0:T(8,128)(2,1)S(1)}, bf16[8,2,32,32]{3,2,1,0:T(8,128)(2,1)}, u32[]{:S(2)}) copy-start(bf16[8,2,32,32]{3,2,1,0:T(8,128)(2,1)} %eig_ref.2) | copy-start | bytes 98308
  15.1 120.8 %copy-start.10 = (s32[8,32]{1,0:T(8,128)S(1)}, s32[8,32]{1,0:T(8,128)}, u32[]{:S(2)}) copy-start(s32[8,32]{1,0:T(8,128)} %mask_ref.2) | copy-start | bytes 3076
  15.1 122.8 %all-to-all-start = ((bf16[32,16,16,256]{3,2,1,0:T(8,128)(2,1)}), bf16[32,16,16,256]{3,2,1,0:T(8,128)(2,1)}, u32[]{:S(2)}, u32[]{:S(2)}) async-start(bf16[32,16,16,256]{3,2,1,0:T(8,128)(2,1)} %shard_map.91), calls=%async_computation | async-start | bytes 8388608 | tf_op jit(solution)/shard_map/all_to_all | solution.py:440
  24.7 120.6 %copy-start.11 = (s32[1,8,32,1]{2,3,1,0:T(1,128)S(1)}, s32[1,8,32,1]{2,3,1,0:T(1,128)}, u32[]{:S(2)}) copy-start(s32[1,8,32,1]{2,3,1,0:T(1,128)} %param.17) | copy-start | bytes 3076
  24.7 120.6 %copy-start.12 = (s32[1,8,32,1]{2,3,1,0:T(1,128)S(1)}, s32[1,8,32,1]{2,3,1,0:T(1,128)}, u32[]{:S(2)}) copy-start(s32[1,8,32,1]{2,3,1,0:T(1,128)} %param.16) | copy-start | bytes 3076
  24.7 49.7 %collective-permute-start.2 = (bf16[16,16,128]{2,1,0:T(8,128)(2,1)S(1)}, bf16[16,16,128]{2,1,0:T(8,128)(2,1)S(1)}, u32[]{:S(2)}, u32[]{:S(2)}) collective-permute-start(bf16[16,16,128]{2,1,0:T(8,128)(2,1)S(1)} %table.1), channel_id=1, source_target_pairs={{0,8},{4,12},{8,16},{12,20},{16,24},{20,28},{24,0},{28,4},{32,40},... | collective-permute-start | bytes 196616 | tf_op jit(solution)/shard_map/ppermute | solution.py:60
  26.2 52.6 %collective-permute-start.1 = (bf16[16,16,128]{2,1,0:T(8,128)(2,1)S(1)}, bf16[16,16,128]{2,1,0:T(8,128)(2,1)S(1)}, u32[]{:S(2)}, u32[]{:S(2)}) collective-permute-start(bf16[16,16,128]{2,1,0:T(8,128)(2,1)S(1)} %table.1), channel_id=1, source_target_pairs={{0,16},{4,20},{8,24},{12,28},{16,0},{20,4},{24,8},{28,12},{32,48},... | collective-permute-start | bytes 196616 | tf_op jit(solution)/shard_map/ppermute | solution.py:60
  28.6 50.2 %collective-permute-start = (bf16[16,16,128]{2,1,0:T(8,128)(2,1)S(1)}, bf16[16,16,128]{2,1,0:T(8,128)(2,1)S(1)}, u32[]{:S(2)}, u32[]{:S(2)}) collective-permute-start(bf16[16,16,128]{2,1,0:T(8,128)(2,1)S(1)} %table.1), channel_id=1, source_target_pairs={{0,24},{4,28},{8,0},{12,4},{16,8},{20,12},{24,16},{28,20},{32,56},... | collective-permute-start | bytes 196616 | tf_op jit(solution)/shard_map/ppermute | solution.py:60
  78.8 8.5 %collective-permute-start.4 = (bf16[4,16,16,128]{3,2,1,0:T(8,128)(2,1)S(1)}, bf16[4,16,16,128]{3,2,1,0:T(8,128)(2,1)S(1)}, u32[]{:S(2)}, u32[]{:S(2)}) collective-permute-start(bf16[4,16,16,128]{3,2,1,0:T(8,128)(2,1)S(1)} %get-tuple-element.26), channel_id=1, source_target_pairs={{0,64},{4,68},{8,72},{12,76},{16,80},{20,84},{24,88},{28,92},{32,9... | collective-permute-start | bytes 786440 | tf_op jit(solution)/shard_map/ppermute | solution.py:60
  81.1 13.1 %collective-permute-start.5 = (bf16[4,16,16,128]{3,2,1,0:T(8,128)(2,1)S(1)}, bf16[4,16,16,128]{3,2,1,0:T(8,128)(2,1)S(1)}, u32[]{:S(2)}, u32[]{:S(2)}) collective-permute-start(bf16[4,16,16,128]{3,2,1,0:T(8,128)(2,1)S(1)} %get-tuple-element.26), channel_id=1, source_target_pairs={{0,32},{4,36},{8,40},{12,44},{16,48},{20,52},{24,56},{28,60},{32,6... | collective-permute-start | bytes 786440 | tf_op jit(solution)/shard_map/ppermute | solution.py:60
  82.1 15.5 %collective-permute-start.3 = (bf16[4,16,16,128]{3,2,1,0:T(8,128)(2,1)S(1)}, bf16[4,16,16,128]{3,2,1,0:T(8,128)(2,1)S(1)}, u32[]{:S(2)}, u32[]{:S(2)}) collective-permute-start(bf16[4,16,16,128]{3,2,1,0:T(8,128)(2,1)S(1)} %get-tuple-element.26), channel_id=1, source_target_pairs={{0,96},{4,100},{8,104},{12,108},{16,112},{20,116},{24,120},{28,124... | collective-permute-start | bytes 786440 | tf_op jit(solution)/shard_map/ppermute | solution.py:60
  94.3 5.8 %collective-permute-start.13 = (bf16[2,4,16,16,128]{4,3,2,1,0:T(8,128)(2,1)S(1)}, bf16[2,4,16,16,128]{4,3,2,1,0:T(8,128)(2,1)S(1)}, u32[]{:S(2)}, u32[]{:S(2)}) collective-permute-start(bf16[2,4,16,16,128]{4,3,2,1,0:T(8,128)(2,1)S(1)} %pad_maximum_fusion.1), channel_id=1, source_target_pairs={{0,4},{4,0},{8,12},{12,8},{16,20},{20,16},{24,28},{28,24},{32,36},... | collective-permute-start | bytes 1572872 | tf_op jit(solution)/shard_map/ppermute | solution.py:60
  94.8 14.7 %collective-permute-start.9 = (bf16[2,4,16,16,128]{4,3,2,1,0:T(8,128)(2,1)S(1)}, bf16[2,4,16,16,128]{4,3,2,1,0:T(8,128)(2,1)S(1)}, u32[]{:S(2)}, u32[]{:S(2)}) collective-permute-start(bf16[2,4,16,16,128]{4,3,2,1,0:T(8,128)(2,1)S(1)} %pad_maximum_fusion.1), channel_id=1, source_target_pairs={{0,1},{1,2},{2,3},{3,0},{4,5},{5,6},{6,7},{7,4},{8,9},{9,10},{10,1... | collective-permute-start | bytes 1572872 | tf_op jit(solution)/shard_map/ppermute | solution.py:64
  96.1 14.8 %collective-permute-start.7 = (bf16[2,4,16,16,128]{4,3,2,1,0:T(8,128)(2,1)S(1)}, bf16[2,4,16,16,128]{4,3,2,1,0:T(8,128)(2,1)S(1)}, u32[]{:S(2)}, u32[]{:S(2)}) collective-permute-start(bf16[2,4,16,16,128]{4,3,2,1,0:T(8,128)(2,1)S(1)} %pad_maximum_fusion.1), channel_id=1, source_target_pairs={{0,3},{1,0},{2,1},{3,2},{4,7},{5,4},{6,5},{7,6},{8,11},{9,8},{10,9... | collective-permute-start | bytes 1572872 | tf_op jit(solution)/shard_map/ppermute | solution.py:64
  97.6 23.0 %collective-permute-start.6 = (bf16[2,4,16,16,128]{4,3,2,1,0:T(8,128)(2,1)S(1)}, bf16[2,4,16,16,128]{4,3,2,1,0:T(8,128)(2,1)}, u32[]{:S(2)}, u32[]{:S(2)}) collective-permute-start(bf16[2,4,16,16,128]{4,3,2,1,0:T(8,128)(2,1)S(1)} %pad_maximum_fusion), channel_id=1, source_target_pairs={{0,3},{1,0},{2,1},{3,2},{4,7},{5,4},{6,5},{7,6},{8,11},{9,8},{10,9... | collective-permute-start | bytes 1572872 | tf_op jit(solution)/shard_map/ppermute | solution.py:64
  99.2 24.1 %collective-permute-start.12 = (bf16[2,4,16,16,128]{4,3,2,1,0:T(8,128)(2,1)S(1)}, bf16[2,4,16,16,128]{4,3,2,1,0:T(8,128)(2,1)S(1)}, u32[]{:S(2)}, u32[]{:S(2)}) collective-permute-start(bf16[2,4,16,16,128]{4,3,2,1,0:T(8,128)(2,1)S(1)} %pad_maximum_fusion), channel_id=1, source_target_pairs={{0,4},{4,0},{8,12},{12,8},{16,20},{20,16},{24,28},{28,24},{32,36},... | collective-permute-start | bytes 1572872 | tf_op jit(solution)/shard_map/ppermute | solution.py:60
  100.1 25.5 %collective-permute-start.11 = (bf16[2,4,16,16,128]{4,3,2,1,0:T(8,128)(2,1)S(1)}, bf16[2,4,16,16,128]{4,3,2,1,0:T(8,128)(2,1)}, u32[]{:S(2)}, u32[]{:S(2)}) collective-permute-start(bf16[2,4,16,16,128]{4,3,2,1,0:T(8,128)(2,1)S(1)} %pad_maximum_fusion), channel_id=1, source_target_pairs={{0,1},{1,2},{2,3},{3,0},{4,5},{5,6},{6,7},{7,4},{8,9},{9,10},{10,1... | collective-permute-start | bytes 1572872 | tf_op jit(solution)/shard_map/ppermute | solution.py:64
  109.6 16.0 %collective-permute-start.19 = (bf16[2,4,16,16,128]{4,3,2,1,0:T(8,128)(2,1)S(1)}, bf16[2,4,16,16,128]{4,3,2,1,0:T(8,128)(2,1)S(1)}, u32[]{:S(2)}, u32[]{:S(2)}) collective-permute-start(bf16[2,4,16,16,128]{4,3,2,1,0:T(8,128)(2,1)S(1)} %collective-permute-done.9), channel_id=1, source_target_pairs={{0,4},{4,0},{8,12},{12,8},{16,20},{20,16},{24,28},{28,24},{32,36},... | collective-permute-start | bytes 1572872 | tf_op jit(solution)/shard_map/ppermute | solution.py:60
  110.9 21.2 %collective-permute-start.10 = (bf16[2,4,16,16,128]{4,3,2,1,0:T(8,128)(2,1)S(1)}, bf16[2,4,16,16,128]{4,3,2,1,0:T(8,128)(2,1)}, u32[]{:S(2)}, u32[]{:S(2)}) collective-permute-start(bf16[2,4,16,16,128]{4,3,2,1,0:T(8,128)(2,1)S(1)} %collective-permute-done.9), channel_id=1, source_target_pairs={{0,1},{1,2},{2,3},{3,0},{4,5},{5,6},{6,7},{7,4},{8,9},{9,10},{10,1... | collective-permute-start | bytes 1572872 | tf_op jit(solution)/shard_map/ppermute | solution.py:64
  120.6 13.1 %collective-permute-start.8 = (bf16[2,4,16,16,128]{4,3,2,1,0:T(8,128)(2,1)}, bf16[2,4,16,16,128]{4,3,2,1,0:T(8,128)(2,1)}, u32[]{:S(2)}, u32[]{:S(2)}) collective-permute-start(bf16[2,4,16,16,128]{4,3,2,1,0:T(8,128)(2,1)} %collective-permute-done.6), channel_id=1, source_target_pairs={{0,3},{1,0},{2,1},{3,2},{4,7},{5,4},{6,5},{7,6},{8,11},{9,8},{10,9... | collective-permute-start | bytes 1572872 | tf_op jit(solution)/shard_map/ppermute | solution.py:64
  123.3 0.8 copy-start.2
  124.1 17.0 %collective-permute-start.15 = (bf16[2,4,16,16,128]{4,3,2,1,0:T(8,128)(2,1)S(1)}, bf16[2,4,16,16,128]{4,3,2,1,0:T(8,128)(2,1)}, u32[]{:S(2)}, u32[]{:S(2)}) collective-permute-start(bf16[2,4,16,16,128]{4,3,2,1,0:T(8,128)(2,1)S(1)} %collective-permute-done.7), channel_id=1, source_target_pairs={{0,4},{4,0},{8,12},{12,8},{16,20},{20,16},{24,28},{28,24},{32,36},... | collective-permute-start | bytes 1572872 | tf_op jit(solution)/shard_map/ppermute | solution.py:60
  125.5 19.1 %collective-permute-start.18 = (bf16[2,4,16,16,128]{4,3,2,1,0:T(8,128)(2,1)}, bf16[2,4,16,16,128]{4,3,2,1,0:T(8,128)(2,1)}, u32[]{:S(2)}, u32[]{:S(2)}) collective-permute-start(bf16[2,4,16,16,128]{4,3,2,1,0:T(8,128)(2,1)} %collective-permute-done.11), channel_id=1, source_target_pairs={{0,4},{4,0},{8,12},{12,8},{16,20},{20,16},{24,28},{28,24},{32,36},... | collective-permute-start | bytes 1572872 | tf_op jit(solution)/shard_map/ppermute | solution.py:60
  125.6 0.8 copy-start.4
  126.4 18.3 %collective-permute-start.14 = (bf16[2,4,16,16,128]{4,3,2,1,0:T(8,128)(2,1)}, bf16[2,4,16,16,128]{4,3,2,1,0:T(8,128)(2,1)}, u32[]{:S(2)}, u32[]{:S(2)}) collective-permute-start(bf16[2,4,16,16,128]{4,3,2,1,0:T(8,128)(2,1)} %collective-permute-done.6), channel_id=1, source_target_pairs={{0,4},{4,0},{8,12},{12,8},{16,20},{20,16},{24,28},{28,24},{32,36},... | collective-permute-start | bytes 1572872 | tf_op jit(solution)/shard_map/ppermute | solution.py:60
  132.1 13.2 %collective-permute-start.17 = (bf16[2,4,16,16,128]{4,3,2,1,0:T(8,128)(2,1)}, bf16[2,4,16,16,128]{4,3,2,1,0:T(8,128)(2,1)}, u32[]{:S(2)}, u32[]{:S(2)}) collective-permute-start(bf16[2,4,16,16,128]{4,3,2,1,0:T(8,128)(2,1)} %collective-permute-done.10), channel_id=1, source_target_pairs={{0,4},{4,0},{8,12},{12,8},{16,20},{20,16},{24,28},{28,24},{32,36},... | collective-permute-start | bytes 1572872 | tf_op jit(solution)/shard_map/ppermute | solution.py:60
  133.7 11.6 %collective-permute-start.16 = (bf16[2,4,16,16,128]{4,3,2,1,0:T(8,128)(2,1)}, bf16[2,4,16,16,128]{4,3,2,1,0:T(8,128)(2,1)}, u32[]{:S(2)}, u32[]{:S(2)}) collective-permute-start(bf16[2,4,16,16,128]{4,3,2,1,0:T(8,128)(2,1)} %collective-permute-done.8), channel_id=1, source_target_pairs={{0,4},{4,0},{8,12},{12,8},{16,20},{20,16},{24,28},{28,24},{32,36},... | collective-permute-start | bytes 1572872 | tf_op jit(solution)/shard_map/ppermute | solution.py:60
  135.8 1.0 copy-start.6
  137.9 7.5 %copy-start.3 = (bf16[2,4,16,16,128]{4,3,2,1,0:T(8,128)(2,1)S(1)}, bf16[2,4,16,16,128]{4,3,2,1,0:T(8,128)(2,1)}, u32[]{:S(2)}) copy-start(bf16[2,4,16,16,128]{4,3,2,1,0:T(8,128)(2,1)} %copy-done.2) | copy-start | bytes 1572868
  137.9 7.5 %copy-start.5 = (bf16[2,4,16,16,128]{4,3,2,1,0:T(8,128)(2,1)S(1)}, bf16[2,4,16,16,128]{4,3,2,1,0:T(8,128)(2,1)}, u32[]{:S(2)}) copy-start(bf16[2,4,16,16,128]{4,3,2,1,0:T(8,128)(2,1)} %copy-done.4) | copy-start | bytes 1572868
  141.1 14.8 %collective-permute-start.20 = (bf16[8,2,32,256]{3,2,1,0:T(8,128)(2,1)S(1)}, bf16[8,2,32,256]{3,2,1,0:T(8,128)(2,1)S(1)}, u32[]{:S(2)}, u32[]{:S(2)}) collective-permute-start(bf16[8,2,32,256]{3,2,1,0:T(8,128)(2,1)S(1)} %get-tuple-element.22), channel_id=1, source_target_pairs={{0,3},{1,0},{2,1},{3,2},{4,7},{5,4},{6,5},{7,6},{8,11},{9,8},{10,9... | collective-permute-start | bytes 786440 | tf_op jit(solution)/shard_map/ppermute | solution.py:64
  144.6 11.3 %collective-permute-start.21 = (bf16[8,2,32,256]{3,2,1,0:T(8,128)(2,1)S(1)}, bf16[8,2,32,256]{3,2,1,0:T(8,128)(2,1)S(1)}, u32[]{:S(2)}, u32[]{:S(2)}) collective-permute-start(bf16[8,2,32,256]{3,2,1,0:T(8,128)(2,1)S(1)} %get-tuple-element.23), channel_id=1, source_target_pairs={{0,2},{1,3},{2,0},{3,1},{4,6},{5,7},{6,4},{7,5},{8,10},{9,11},{10,... | collective-permute-start | bytes 786440 | tf_op jit(solution)/shard_map/ppermute | solution.py:64
  144.6 14.9 %collective-permute-start.22 = (bf16[8,2,32,256]{3,2,1,0:T(8,128)(2,1)S(1)}, bf16[8,2,32,256]{3,2,1,0:T(8,128)(2,1)S(1)}, u32[]{:S(2)}, u32[]{:S(2)}) collective-permute-start(bf16[8,2,32,256]{3,2,1,0:T(8,128)(2,1)S(1)} %get-tuple-element.24), channel_id=1, source_target_pairs={{0,1},{1,2},{2,3},{3,0},{4,5},{5,6},{6,7},{7,4},{8,9},{9,10},{10,1... | collective-permute-start | bytes 786440 | tf_op jit(solution)/shard_map/ppermute | solution.py:64
